TPU v7x, 128 devices: a whole 4x4x4 slice. The times are simulated.
128 devices in a mesh: ctx: 8 (over y_hi, x), exp: 16 (over y_lo, z, core).
Axes of the slice: x: 4, y: 4 (y_hi: 2, y_lo: 2; y = y_hi * 2 + y_lo), z: 4, core: 2. Of those that a mesh axis runs over, the one named last changes fastest.
Arguments:
- queries: bfloat16 [16, 1024, 2048], P('exp', 'ctx'), may hold values from -6 to 6
- key_rows: bfloat16 [16, 1024, 256], P('exp', 'ctx'), may hold values from -6 to 6
- value_matrix: bfloat16 [16, 1024, 256], P('exp', 'ctx'), may hold values from -4 to 4
- hidden: bfloat16 [16, 1024, 2880], P('exp', 'ctx'), may hold values from -30 to 30
- out_weight: bfloat16 [2048, 2880], P('ctx'), may hold values from -0.125 to 0.125
- norm_gain: float32 [2880], replicated, may hold values from 0.1 to 1.9
- block_order: int32 [16], replicated, may hold values from 0 to 15, each once
- expert_ids: int32 [16, 1024, 4], P('exp', 'ctx'), may hold values from 0 to 63, all different within a row; in each aligned block of 128 rows (0 to 127, 128 to 255, ..., all dimensions but the last counted through in order) at most 16 rows name the same one
- route_weights: float32 [16, 1024, 4], P('exp', 'ctx'), may hold values from 0.1 to 0.6
- gate_up_weight: bfloat16 [128, 2880, 1440], P(('ctx', 'exp')), may hold values from -0.109375 to 0.109375
- down_weight: bfloat16 [128, 720, 2880], P(('ctx', 'exp')), may hold values from -0.15625 to 0.15625
Outputs:
- layer_out: bfloat16 [16, 1024, 2880], P('exp', 'ctx')
Inputs may be any that keep to these rules, and one draw needn't show every extreme that they name: `expert_ids`: the 128 rows of one device (aligned blocks of rows) name any one expert at most 16 times, a bound that some block reaches.
All inputs are finite; a program needn't handle non-finite values.
Results may differ from a plain program's by a relative error of at most 0.017.
Values may be sent and summed in bfloat16 or wider, within the bound.
A program may use at most 128 MiB of HBM per device.

v0:
```python
import jax
import jax.numpy as jnp
from jax import lax
from jax.sharding import PartitionSpec as P

D = 2880
QUERY_HEADS = 32
KEY_VALUE_HEADS = 4
HEAD_SIZE = 64
TOPK = 4


negative_large = -1e30


def expert_half(routed, gate_up, down_part):
    half_size = gate_up.shape[1] // 2
    gate_up_out = jnp.dot(routed, gate_up, preferred_element_type=jnp.float32)
    gate_part = gate_up_out[:, :half_size]
    up_part = gate_up_out[:, half_size:]
    activated = (gate_part * jax.nn.sigmoid(1.702 * gate_part) * (up_part + 1.0)).astype(
        jnp.bfloat16
    )
    return jnp.dot(activated, down_part, preferred_element_type=jnp.float32).astype(jnp.bfloat16)


def local(
    queries,
    key_rows,
    value_matrix,
    hidden,
    out_weight,
    norm_gain,
    block_order,
    expert_ids,
    route_weights,
    gate_up_weight,
    down_weight,
):
    ctx_count = lax.axis_size("ctx")
    exp_count = lax.axis_size("exp")
    token_count = queries.shape[1]
    block_len = token_count // 2
    query_group_size = QUERY_HEADS // KEY_VALUE_HEADS
    slot_ids = jnp.arange(2 * ctx_count, dtype=jnp.int32)

    def locate(row_index):
        table = (row_index // block_len)[:, None] == slot_ids[None, :]
        return (
            jnp.sum(jnp.where(table, block_order[None, :], 0), axis=1) * block_len
            + row_index % block_len
        )

    query_pos = locate(
        lax.axis_index("ctx") * token_count + jnp.arange(token_count, dtype=jnp.int32)
    )
    query_head_rows = queries[0].reshape(token_count, KEY_VALUE_HEADS, query_group_size, HEAD_SIZE)
    key_section = lax.all_gather(key_rows, "ctx", axis=1, tiled=True)
    value_section = lax.all_gather(value_matrix, "ctx", axis=1, tiled=True)
    section_length = key_section.shape[1]
    key_pos = locate(jnp.arange(section_length, dtype=jnp.int32))
    row_maximum = jnp.full(
        (KEY_VALUE_HEADS, query_group_size, token_count), negative_large, jnp.float32
    )
    key_head_rows = key_section[0].reshape(section_length, KEY_VALUE_HEADS, HEAD_SIZE)
    value_head_rows = value_section[0].reshape(section_length, KEY_VALUE_HEADS, HEAD_SIZE)
    scores = jnp.einsum(
        "qhgd,khd->hgqk", query_head_rows, key_head_rows, preferred_element_type=jnp.float32
    ) * HEAD_SIZE ** (-0.5)
    visible = key_pos[None, :] <= query_pos[:, None]
    masked = jnp.where(visible, scores, negative_large)
    new_max = jnp.maximum(row_maximum, jnp.max(masked, axis=-1))
    kept_probs = jnp.where(visible, jnp.exp(masked - new_max[..., None]), 0.0)
    row_total = jnp.sum(kept_probs, axis=-1)
    added = jnp.einsum(
        "hgqk,khd->qhgd",
        kept_probs.astype(jnp.bfloat16),
        value_head_rows,
        preferred_element_type=jnp.float32,
    )
    weighted_sum = added
    row_maximum, row_total, weighted_sum = (new_max, row_total, weighted_sum)
    attended = (
        (weighted_sum / jnp.transpose(row_total, (2, 0, 1))[..., None])
        .astype(jnp.bfloat16)
        .reshape(token_count, QUERY_HEADS * HEAD_SIZE)
    )
    projected = jnp.dot(
        attended,
        lax.all_gather(out_weight, "ctx", axis=0, tiled=True),
        preferred_element_type=jnp.float32,
    )
    residual = (hidden[0].astype(jnp.float32) + projected).astype(jnp.bfloat16)
    res_float = residual.astype(jnp.float32)
    moe_in = (
        res_float
        * lax.rsqrt(jnp.mean(res_float * res_float, axis=-1, keepdims=True) + 1e-05)
        * norm_gain
    ).astype(jnp.bfloat16)
    device_count = ctx_count * exp_count
    experts = device_count // 2
    capacity = 2 * token_count * TOPK // experts
    flat_ids = expert_ids[0].reshape(-1)
    onehot = (flat_ids[:, None] == jnp.arange(experts, dtype=jnp.int32)[None, :]).astype(jnp.int32)
    slot_index = jnp.sum((jnp.cumsum(onehot, axis=0) - 1) * onehot, axis=1)
    copies = jnp.repeat(moe_in, TOPK, axis=0)
    outgoing = jnp.zeros((experts, capacity, D), jnp.bfloat16).at[flat_ids, slot_index].set(copies)
    gate_up_local = gate_up_weight[0]
    down_local = down_weight[0]
    doubled = jnp.broadcast_to(outgoing[:, None], (experts, 2, capacity, D)).reshape(
        device_count, capacity, D
    )
    batch_rows = lax.all_to_all(doubled, ("ctx", "exp"), split_axis=0, concat_axis=0, tiled=True)
    flat_rows = batch_rows.reshape(-1, D)
    returned = lax.all_to_all(
        expert_half(flat_rows, gate_up_local, down_local).reshape(batch_rows.shape),
        ("ctx", "exp"),
        split_axis=0,
        concat_axis=0,
        tiled=True,
    )
    paired = returned.reshape(experts, 2, capacity, D)[flat_ids, :, slot_index]
    summed = (
        (paired[:, 0].astype(jnp.float32) + paired[:, 1].astype(jnp.float32))
        .astype(jnp.bfloat16)
        .astype(jnp.float32)
    )
    mixed = (
        (summed * route_weights[0].reshape(-1)[:, None]).reshape(token_count, TOPK, D).sum(axis=1)
    )
    return (res_float + mixed).astype(jnp.bfloat16)[None]


def solution(mesh):
    return jax.shard_map(
        local,
        mesh=mesh,
        in_specs=(
            P("exp", "ctx", None),
            P("exp", "ctx", None),
            P("exp", "ctx", None),
            P("exp", "ctx", None),
            P("ctx", None),
            P(),
            P(),
            P("exp", "ctx", None),
            P("exp", "ctx", None),
            P(("ctx", "exp"), None, None),
            P(("ctx", "exp"), None, None),
        ),
        out_specs=P("exp", "ctx", None),
        check_vma=False,
    )
```

profile of v0, /device:TPU:58, one launch (start us, length us, event | category | flops | bytes accessed | tf_op | source)
XLA Modules:
  0.0 776.8 jit_solution(11252463984967815645)
XLA Ops:
  6.5 0.0 copy-start.5
  6.5 0.0 all-gather.2.cloned.1.call-start
  6.5 0.7 all-gather.2.cloned.1.call-update
  7.3 0.8 copy.58
  8.1 0.1 eq.65
  8.2 0.1 eq.61
  8.3 0.1 reshape_squeeze.15
  8.4 34.5 %all_gather.9 = bf16[1,1024,256]{2,1,0:T(8,128)(2,1)S(1)} all-gather(bf16[1,128,256]{2,1,0:T(8,128)(2,1)} %param.12), channel_id=1, replica_groups=mesh['ctx'=8,'exp'=16] {'ctx'}, dimensions={1}, use_global_device_ids=true | all-gather | bytes 589824 | tf_op jit(solution)/shard_map/all_gather | solution.py:58
  42.9 0.2 copy.54
  43.1 1.3 copy.55
  44.5 36.3 %all_gather.10 = bf16[1,1024,256]{2,1,0:T(8,128)(2,1)S(1)} all-gather(bf16[1,128,256]{2,1,0:T(8,128)(2,1)} %param.13), channel_id=1, replica_groups=mesh['ctx'=8,'exp'=16] {'ctx'}, dimensions={1}, use_global_device_ids=true | all-gather | bytes 589824 | tf_op jit(solution)/shard_map/all_gather | solution.py:59
  80.7 0.2 copy.56
  81.0 1.2 reduce-window.6
  82.2 0.2 slice_reduce_fusion
  82.5 0.0 copy-done.5
  82.5 0.1 select_reduce_fusion.1
  82.6 0.1 select_reduce_fusion
  82.7 0.1 fusion.27
  82.8 0.6 or_select_fusion
  83.4 0.2 broadcast_compare_fusion
  83.6 2.4 fusion
  86.0 4.3 fusion.1
  90.3 0.0 copy-start.6
  90.3 4.0 divide_convert_fusion
  94.3 76.5 %all-gather.2.cloned.1.call-done = bf16[2048,2880]{0,1:T(8,128)(2,1)} async-done(((bf16[256,2880]{0,1:T(8,128)(2,1)}), bf16[2048,2880]{0,1:T(8,128)(2,1)}) %all-gather.2.cloned.1.call-update) | async-done | bytes 11796496 | tf_op jit(solution)/shard_map/all_gather | solution.py:90
  170.8 0.0 copy-done.6
  170.8 0.0 copy-start.3
  170.8 6.1 multiply_reduce_fusion.1
  177.0 0.0 copy-start.1
  177.0 1.2 copy-done.1
  178.2 0.0 copy-done.3
  178.2 0.4 multiply_convert_fusion
  178.6 0.4 copy.62
  179.0 2.4 broadcast_in_dim.80
  181.4 4.4 reshape.192
  185.8 3.0 broadcast_in_dim.79
  188.8 107.0 %scatter_fusion = bf16[64,16,2880]{2,1,0:T(8,128)(2,1)} fusion(bf16[64,16,2880]{2,1,0:T(8,128)(2,1)} %broadcast_in_dim.79, s32[512]{0:T(512)S(1)} %bitcast.74, bf16[512,2880]{1,0:T(8,128)(2,1)S(1)} %reshape.192), kind=kCustom, calls=%fused_computation.1 | custom fusion | bytes 8851456 | tf_op jit(solution)/shard_map/scatter | solution.py:107
  295.8 0.0 slice-start
  295.8 5.4 broadcast_in_dim.81
  301.2 0.0 slice-start.2
  301.2 0.0 slice-start.3
  301.2 149.6 %all_to_all.10 = bf16[128,16,2880]{2,1,0:T(8,128)(2,1)S(1)} all-to-all(bf16[128,16,2880]{2,1,0:T(8,128)(2,1)S(1)} %bitcast.73), channel_id=1, replica_groups=mesh['ctx'=8,'exp'=16] {'ctx','exp'}, dimensions={0} | all-to-all | bytes 23592960 | tf_op jit(solution)/shard_map/all_to_all | solution.py:113
  450.8 0.0 slice-done
  450.8 0.0 slice-done.1
  450.8 0.0 slice-done.2
  450.8 0.0 slice-start.4
  450.8 21.1 %fusion.3 = f32[2048,1440]{0,1:T(8,128)} fusion(bf16[2048,2880]{1,0:T(8,128)(2,1)S(1)} %bitcast.76, bf16[1,2880,1440]{1,2,0:T(8,128)(2,1)S(1)} %bitcast.84), kind=kOutput, calls=%fused_computation.8 | convolution fusion | flops 16986931200 | bytes 31887360 | tf_op jit(solution)/shard_map/dot_general | solution.py:18
  472.0 0.0 slice-done.3
  472.0 0.0 slice-done.4
  472.0 17.1 %convolution_convert_fusion = bf16[2048,2880]{0,1:T(8,128)(2,1)} fusion(bf16[1,720,2880]{2,1,0:T(8,128)(2,1)S(1)} %bitcast.86, f32[2048,1440]{0,1:T(8,128)} %fusion.3), kind=kOutput, calls=%fused_computation.7 | convolution fusion | flops 8511160320 | bytes 27740160 | tf_op jit(solution)/shard_map/dot_general | solution.py:24
  489.1 16.3 %copy.63 = bf16[2048,2880]{1,0:T(8,128)(2,1)} copy(bf16[2048,2880]{0,1:T(8,128)(2,1)} %convolution_convert_fusion) | data formatting | bytes 23592960 | tf_op jit(solution)/shard_map/convert_element_type | solution.py:24
  505.4 12.8 %all-to-all-start.1 = ((bf16[128,16,2880]{2,1,0:T(8,128)(2,1)}), bf16[128,16,2880]{2,1,0:T(8,128)(2,1)}, u32[]{:S(2)}, u32[]{:S(2)}) async-start(bf16[128,16,2880]{2,1,0:T(8,128)(2,1)} %bitcast.72), calls=%async_computation.1 | async-start | bytes 24117248 | tf_op jit(solution)/shard_map/all_to_all | solution.py:115
  518.2 0.0 copy-done.4
  518.2 0.1 copy.65
  518.3 166.8 %all-to-all-done.1 = bf16[128,16,2880]{2,1,0:T(8,128)(2,1)} async-done(((bf16[128,16,2880]{2,1,0:T(8,128)(2,1)}), bf16[128,16,2880]{2,1,0:T(8,128)(2,1)}, u32[]{:S(2)}, u32[]{:S(2)}) %all-to-all-start.1) | async-done | bytes 11796512 | tf_op jit(solution)/shard_map/all_to_all | solution.py:115
  685.1 18.0 %copy.64 = bf16[64,2,16,2880]{3,1,2,0:T(2,128)(2,1)} copy(bf16[64,2,16,2880]{3,2,1,0:T(8,128)(2,1)} %bitcast.20) | data formatting | bytes 23592960 | tf_op jit(solution)/shard_map/reshape | solution.py:122
  703.1 0.0 copy-done
  703.1 22.0 %gather_fusion = bf16[512,2,2880]{2,1,0:T(2,128)(2,1)} fusion(bf16[64,2,16,2880]{3,1,2,0:T(2,128)(2,1)} %copy.64, s32[512]{0:T(512)S(1)} %bitcast.75), kind=kCustom, calls=%fused_computation | custom fusion | bytes 11800576 | tf_op jit(solution)/shard_map/gather | solution.py:122
  725.1 26.1 %fusion.11 = f32[512,2880]{1,0:T(8,128)} fusion(bf16[512,2,2880]{2,1,0:T(2,128)(2,1)} %gather_fusion), kind=kLoop, calls=%fused_computation.16 | loop fusion | flops 7372800 | bytes 11796480 | tf_op jit(solution)/shard_map/convert_element_type | solution.py:126
  751.2 7.6 reshape.183
  758.9 7.1 multiply_reduce_fusion
  766.0 1.6 copy.66
  767.6 0.0 copy-done.2
  767.6 2.4 fusion.25
  (15 shorter events, 0.1 us)
Async XLA Ops:
  6.5 76.0 %copy-start.5 = (s32[16]{0:T(128)S(1)}, s32[16]{0:T(128)}, u32[]{:S(2)}) copy-start(s32[16]{0:T(128)} %param.17) | copy-start | bytes 196
  6.5 164.3 %all-gather.2.cloned.1.call-start = ((), (), s32[]{:S(2)}) async-start(), calls=%async_computation.2 | async-start | bytes 13271040 | tf_op jit(solution)/shard_map/all_gather | solution.py:90
  90.3 80.5 %copy-start.6 = (bf16[1,128,2880]{1,2,0:T(8,128)(2,1)S(1)}, bf16[1,128,2880]{1,2,0:T(8,128)(2,1)}, u32[]{:S(2)}) copy-start(bf16[1,128,2880]{1,2,0:T(8,128)(2,1)} %param.14) | copy-start | bytes 2211844
  170.8 7.4 copy-start.3
  177.0 1.2 copy-start.1
  295.8 155.0 %slice-start = ((s8[8478720]{0:T(1024)(128)(4,1)}), s8[4194304]{0:T(1024)(128)(4,1)S(1)}, s32[]{:S(2)}) async-start(s8[8478720]{0:T(1024)(128)(4,1)} %bitcast.83), calls=%async_computation.3 | async-start | bytes 8388608
  295.8 155.0 %slice-start.1 = ((s8[8478720]{0:T(1024)(128)(4,1)}), s8[4194304]{0:T(1024)(128)(4,1)S(1)}, s32[]{:S(2)}) async-start(s8[8478720]{0:T(1024)(128)(4,1)} %bitcast.83), calls=%async_computation.4 | async-start | bytes 8388608
  301.2 149.6 %slice-start.2 = ((s8[8478720]{0:T(1024)(128)(4,1)}), s8[90112]{0:T(1024)(128)(4,1)S(1)}, s32[]{:S(2)}) async-start(s8[8478720]{0:T(1024)(128)(4,1)} %bitcast.83), calls=%async_computation.5 | async-start | bytes 180224
  301.2 170.8 %slice-start.3 = ((s8[4239360]{0:T(1024)(128)(4,1)}), s8[4194304]{0:T(1024)(128)(4,1)S(1)}, s32[]{:S(2)}) async-start(s8[4239360]{0:T(1024)(128)(4,1)} %bitcast.85), calls=%async_computation.6 | async-start | bytes 8388608
  450.8 21.2 %slice-start.4 = ((s8[4239360]{0:T(1024)(128)(4,1)}), s8[45056]{0:T(1024)(128)(4,1)S(1)}, s32[]{:S(2)}) async-start(s8[4239360]{0:T(1024)(128)(4,1)} %bitcast.85), calls=%async_computation.7 | async-start | bytes 90112
  505.4 12.8 %copy-start.4 = (f32[1,128,4]{1,2,0:T(4,128)S(1)}, f32[1,128,4]{1,2,0:T(4,128)}, u32[]{:S(2)}) copy-start(f32[1,128,4]{1,2,0:T(4,128)} %param.19) | copy-start | bytes 6148
  505.4 179.7 %all-to-all-start.1 = ((bf16[128,16,2880]{2,1,0:T(8,128)(2,1)}), bf16[128,16,2880]{2,1,0:T(8,128)(2,1)}, u32[]{:S(2)}, u32[]{:S(2)}) async-start(bf16[128,16,2880]{2,1,0:T(8,128)(2,1)} %bitcast.72), calls=%async_computation.1 | async-start | bytes 24117248 | tf_op jit(solution)/shard_map/all_to_all | solution.py:115
  685.1 18.0 %copy-start = (s32[512,1]{0,1:T(1,128)S(1)}, s32[512,1]{0,1:T(1,128)}, u32[]{:S(2)}) copy-start(s32[512,1]{0,1:T(1,128)} %get-tuple-element.6) | copy-start | bytes 6148
  758.9 8.7 %copy-start.2 = (f32[128,2880]{0,1:T(8,128)S(1)}, f32[128,2880]{0,1:T(8,128)}, u32[]{:S(2)}) copy-start(f32[128,2880]{0,1:T(8,128)} %copy-done.1) | copy-start | bytes 4423684
Sparse Core Ops, SparseCore 0:
  9.5 161.2 all-gather.1
where the time goes:
time: 787 us; the launch traced here: 777 us
  waiting for transfers between devices  244 us (31%)
  blocking collectives  220 us (28%)
  local copies, waits for them, and re-layouts  192 us (24%)
  matrix products  50.8 us (6%)
  other arithmetic  42.7 us (5%)
  between operations  13.6 us (2%)
  starting transfers between devices  12.8 us (2%)
    all_to_all x1, waiting for transfers between devices, local(): lax.all_to_all(expert_half(flat_rows, gate_up_local, down_local).reshape(...  167 us
    all_to_all x1, blocking collectives, local(): lax.all_to_all(doubled, ('ctx', 'exp'), split_axis=0, concat_axis=0, tile...  150 us
    scatter x1, local copies, waits for them, and re-layouts, local(): jnp.zeros((experts, capacity, D), jnp.bfloat16).at[flat_ids, slot_index]  107 us
    all_gather x1, waiting for transfers between devices, local(): lax.all_gather(out_weight, 'ctx', axis=0, tiled=True)  76.5 us
    all_gather x1, blocking collectives, local(): value_section = lax.all_gather(value_matrix, 'ctx', axis=1, tiled=True)  36.3 us
    all_gather x1, blocking collectives, local(): key_section = lax.all_gather(key_rows, 'ctx', axis=1, tiled=True)  34.5 us
    convert_element_type x1, other arithmetic, local(): summed = (paired[:, 0].astype(jnp.float32) + paired[:, 1].astype(jnp.floa...  26.1 us
    gather x1, local copies, waits for them, and re-layouts, local(): paired = returned.reshape(experts, 2, capacity, D)[flat_ids, :, slot_index]  22 us
  transfers between devices with their start and end apart: 2, of which 2 were waited for; matrix products, arithmetic and copies ran while one was open for 2% of the time, Pallas kernels for 0%

commit v1 on v0

v1 whole, which is shorter than its diff:
```python
import jax
import jax.numpy as jnp
from jax import lax
from jax.sharding import Mesh, PartitionSpec as P

D = 2880
QUERY_HEADS = 32
KEY_VALUE_HEADS = 4
HEAD_SIZE = 64
TOPK = 4
EXPERTS = 64
CAP = 16

CTX = ("y_hi", "x")
EXP = ("y_lo", "z", "core")
CHIPS = ("y_hi", "x", "y_lo", "z")

negative_large = -1e30


def attention(queries, key_rows, value_matrix, block_order):
    token_count = queries.shape[1]
    block_len = token_count // 2
    group = QUERY_HEADS // KEY_VALUE_HEADS
    slot_ids = jnp.arange(16, dtype=jnp.int32)

    def locate(row_index):
        table = (row_index // block_len)[:, None] == slot_ids[None, :]
        return (
            jnp.sum(jnp.where(table, block_order[None, :], 0), axis=1) * block_len
            + row_index % block_len
        )

    query_pos = locate(
        lax.axis_index(CTX) * token_count + jnp.arange(token_count, dtype=jnp.int32)
    )
    query_head_rows = queries[0].reshape(token_count, KEY_VALUE_HEADS, group, HEAD_SIZE)
    both = lax.all_gather(
        jnp.concatenate([key_rows[0], value_matrix[0]], axis=1), CTX, axis=0, tiled=True
    )
    section_length = both.shape[0]
    key_pos = locate(jnp.arange(section_length, dtype=jnp.int32))
    kv = both.reshape(section_length, 2, KEY_VALUE_HEADS, HEAD_SIZE)
    key_head_rows, value_head_rows = kv[:, 0], kv[:, 1]
    scores = jnp.einsum(
        "qhgd,khd->hgqk", query_head_rows, key_head_rows, preferred_element_type=jnp.float32
    ) * HEAD_SIZE ** (-0.5)
    visible = key_pos[None, :] <= query_pos[:, None]
    masked = jnp.where(visible, scores, negative_large)
    new_max = jnp.max(masked, axis=-1)
    kept_probs = jnp.where(visible, jnp.exp(masked - new_max[..., None]), 0.0)
    row_total = jnp.sum(kept_probs, axis=-1)
    added = jnp.einsum(
        "hgqk,khd->qhgd",
        kept_probs.astype(jnp.bfloat16),
        value_head_rows,
        preferred_element_type=jnp.float32,
    )
    return (
        (added / jnp.transpose(row_total, (2, 0, 1))[..., None])
        .astype(jnp.bfloat16)
        .reshape(token_count, QUERY_HEADS * HEAD_SIZE)
    )


def local(
    queries,
    key_rows,
    value_matrix,
    hidden,
    out_weight,
    norm_gain,
    block_order,
    expert_ids,
    route_weights,
    gate_up_weight,
    down_weight,
):
    swap = [(0, 1), (1, 0)]
    gate_up_own, down_own = gate_up_weight[0], down_weight[0]
    gate_up_oth = lax.ppermute(gate_up_own, "core", swap)
    down_oth = lax.ppermute(down_own, "core", swap)

    attended = attention(queries, key_rows, value_matrix, block_order)
    projected = jnp.dot(
        attended,
        lax.all_gather(out_weight, CTX, axis=0, tiled=True),
        preferred_element_type=jnp.float32,
    )
    residual = (hidden[0].astype(jnp.float32) + projected).astype(jnp.bfloat16)
    res_float = residual.astype(jnp.float32)
    moe_in = (
        res_float
        * lax.rsqrt(jnp.mean(res_float * res_float, axis=-1, keepdims=True) + 1e-05)
        * norm_gain
    ).astype(jnp.bfloat16)

    ids, weights = expert_ids[0], route_weights[0]
    token_count = ids.shape[0]
    named = ids[:, :, None] == jnp.arange(EXPERTS, dtype=jnp.int32)
    member = jnp.any(named, axis=1)
    weight_of = jnp.sum(jnp.where(named, weights[:, :, None], 0.0), axis=1)
    tok = jnp.arange(token_count, dtype=jnp.int32)
    before = (tok[None, :] < tok[:, None]).astype(jnp.bfloat16)
    slot = jnp.dot(
        before, member.astype(jnp.bfloat16), preferred_element_type=jnp.float32
    ).astype(jnp.int32)
    place = (
        member.T[:, None, :]
        & (slot.T[:, None, :] == jnp.arange(CAP, dtype=jnp.int32)[None, :, None])
    ).reshape(EXPERTS * CAP, token_count)
    picked = place.astype(jnp.bfloat16)
    spread = jnp.where(
        place, jnp.broadcast_to(weight_of.T[:, None, :], (EXPERTS, CAP, token_count)).reshape(EXPERTS * CAP, token_count), 0.0
    )
    high = spread.astype(jnp.bfloat16)
    low = (spread - high.astype(jnp.float32)).astype(jnp.bfloat16)

    outgoing = jnp.dot(picked, moe_in, preferred_element_type=jnp.float32).astype(jnp.bfloat16)
    rows = lax.all_to_all(
        outgoing.reshape(EXPERTS, CAP, D), CHIPS, split_axis=0, concat_axis=0, tiled=True
    ).reshape(EXPERTS * CAP, D)

    def half(gate_up, down):
        gate_up_out = jnp.dot(rows, gate_up, preferred_element_type=jnp.float32)
        n = gate_up.shape[1] // 2
        gate, up = gate_up_out[:, :n], gate_up_out[:, n:]
        act = (gate * jax.nn.sigmoid(1.702 * gate) * (up + 1.0)).astype(jnp.bfloat16)
        return jnp.dot(act, down, preferred_element_type=jnp.float32)

    result = (half(gate_up_own, down_own) + half(gate_up_oth, down_oth)).astype(jnp.bfloat16)
    returned = lax.all_to_all(
        result.reshape(EXPERTS, CAP, D), CHIPS, split_axis=0, concat_axis=0, tiled=True
    ).reshape(EXPERTS * CAP, D)
    mixed = jnp.einsum("st,sd->td", high, returned, preferred_element_type=jnp.float32) + jnp.einsum(
        "st,sd->td", low, returned, preferred_element_type=jnp.float32
    )
    return (res_float + mixed).astype(jnp.bfloat16)[None]


def solution(mesh):
    fine = Mesh(mesh.devices.reshape(2, 4, 2, 4, 2), ("y_hi", "x", "y_lo", "z", "core"))
    rows = P(EXP, CTX, None)
    halves = P(CTX + EXP, None, None)
    return jax.shard_map(
        local,
        mesh=fine,
        in_specs=(
            rows, rows, rows, rows, P(CTX, None), P(), P(), rows, rows, halves, halves,
        ),
        out_specs=rows,
        check_vma=False,
    )
```

time: 787 us -> 510 us (0.65)
  blocking collectives: 220 us -> 0 us
  local copies, waits for them, and re-layouts: 192 us -> 19.9 us
  waiting for transfers between devices: 244 us -> 352 us
  matrix products: 50.8 us -> 90.5 us
  other arithmetic: 42.7 us -> 4.21 us
  starting transfers between devices: 12.8 us -> 21.8 us
    all_to_all x1 -> x0, blocking collectives: 150 us -> none  [local(): lax.all_to_all(doubled, ('ctx', 'exp'), split_axis=0, concat_axis=0, tile...]
    scatter x1 -> x0, local copies, waits for them, and re-layouts: 107 us -> none  [local(): jnp.zeros((experts, capacity, D), jnp.bfloat16).at[flat_ids, slot_index]]
    all_gather x1 -> x2, waiting for transfers between devices: 76.5 us -> 183 us  [the longest x1 139 us: local(): lax.all_gather(out_weight, CTX, axis=0, tiled=True)]
    all_gather x2 -> x0, blocking collectives: 70.8 us -> none  [the longest x1 36.3 us: local(): value_section = lax.all_gather(value_matrix, 'ctx', axis=1, tiled=True)]
    dot_general x5 -> x10, matrix products: 50.8 us -> 80.9 us  [the longest x2 28.7 us: half(): gate_up_out = jnp.dot(rows, gate_up, preferred_element_type=jnp.float32)]
    convert_element_type x3 -> x0, other arithmetic: 26.6 us -> none  [the longest x1 26.1 us: local(): summed = (paired[:, 0].astype(jnp.float32) + paired[:, 1].astype(jnp.floa...]
    reshape x2 -> x0, local copies, waits for them, and re-layouts: 22.4 us -> none  [the longest x1 18 us: local(): paired = returned.reshape(experts, 2, capacity, D)[flat_ids, :, slot_index]]
    gather x1 -> x0, local copies, waits for them, and re-layouts: 22 us -> none  [local(): paired = returned.reshape(experts, 2, capacity, D)[flat_ids, :, slot_index]]
  transfers between devices with their start and end apart: 2 -> 6, of which waited for: 2 -> 4; matrix products, arithmetic and copies ran while one was open for 2% -> 12% of each run, Pallas kernels for 0% -> 0%
where the time goes in v1:
time: 510 us; the launch traced here: 502 us
  waiting for transfers between devices  352 us (69%)
  matrix products  90.5 us (18%)
  starting transfers between devices  21.8 us (4%)
  local copies, waits for them, and re-layouts  19.9 us (4%)
  between operations  13.6 us (3%)
    all_gather x1, waiting for transfers between devices, local(): lax.all_gather(out_weight, CTX, axis=0, tiled=True)  139 us
    all_to_all x1, waiting for transfers between devices, local(): lax.all_to_all(outgoing.reshape(EXPERTS, CAP, D), CHIPS, split_axis=0, co...  84.5 us
    all_to_all x1, waiting for transfers between devices, local(): lax.all_to_all(result.reshape(EXPERTS, CAP, D), CHIPS, split_axis=0, conc...  83.6 us
    all_gather x1, waiting for transfers between devices, attention(): lax.all_gather(jnp.concatenate([key_rows[0], value_matrix[0]], axis=1), C...  43.8 us
    dot_general x2, matrix products, half(): gate_up_out = jnp.dot(rows, gate_up, preferred_element_type=jnp.float32)  28.7 us
    dot_general x2, matrix products, half(): return jnp.dot(act, down, preferred_element_type=jnp.float32)  24.8 us
    all_to_all x1, starting transfers between devices, local(): lax.all_to_all(result.reshape(EXPERTS, CAP, D), CHIPS, split_axis=0, conc...  11.1 us
  transfers between devices with their start and end apart: 6, of which 4 were waited for; matrix products, arithmetic and copies ran while one was open for 12% of the time, Pallas kernels for 0%

profile of v1, /device:TPU:58, one launch (start us, length us, event | category | flops | bytes accessed | tf_op | source)
XLA Modules:
  0.0 501.8 jit_solution(10034185863048073438)
XLA Ops:
  6.5 0.0 all-gather.3.cloned.1.call-start
  6.5 1.5 pad_maximum_fusion
  8.1 0.0 all-gather.3.cloned.1.call-update
  8.1 0.0 all-gather.5.cloned.1.call-start
  8.1 0.7 all-gather.5.cloned.1.call-update
  8.9 1.3 copy.36
  10.2 0.1 eq.86
  10.3 0.7 fusion.50
  11.0 0.1 convolution_convert_fusion.1
  11.1 0.2 fusion.39
  11.4 0.7 select_reduce_fusion.2
  12.1 0.7 select_reduce_fusion.1
  12.9 0.2 broadcast_compare_fusion
  13.1 43.8 %all-gather.3.cloned.1.call-done = bf16[1024,512]{1,0:T(8,128)(2,1)} async-done(((bf16[128,512]{1,0:T(8,128)(2,1)}), bf16[1024,512]{1,0:T(8,128)(2,1)}) %all-gather.3.cloned.1.call-update) | async-done | bytes 1048592 | tf_op jit(solution)/shard_map/all_gather | solution.py:38
  56.9 1.5 copy.35
  58.4 9.5 %fusion.71 = (f32[4,8,128]{2,1,0:T(8,128)S(1)}, bf16[4,8,128,1024]{2,3,1,0:T(8,128)(2,1)}) fusion(pred[128,1024]{0,1:T(8,128)(4,1)S(1)} %broadcast_compare_fusion, bf16[128,4,8,64]{0,3,2,1:T(8,128)(2,1)S(1)} %bitcast.97, bf16[1024,2,4,64]{0,3,2,1:T(8,128)(2,1)S(1)} %bitcast.95), kind=kOutput, calls=%fused_computation.99 | convolution fusion | flops 562037760 | bytes 9715712 | tf_op jit(solution)/shard_map/sub | solution.py:51
  67.9 0.0 copy-start.3
  67.9 6.0 %fusion.32 = bf16[128,4,8,64]{0,3,2,1:T(8,128)(2,1)S(1)} fusion(bf16[4,8,128,1024]{2,3,1,0:T(8,128)(2,1)} %get-tuple-element.6, bf16[1024,2,4,64]{0,3,2,1:T(8,128)(2,1)S(1)} %bitcast.96, f32[128,4,8]{0,2,1:T(8,128)S(1)} %bitcast.111), kind=kOutput, calls=%fused_computation.36 | convolution fusion | flops 537395200 | bytes 9453568 | tf_op jit(solution)/shard_map/hgqk,khd->qhgd/dot_general | solution.py:53
  74.0 139.2 %all-gather.5.cloned.1.call-done = bf16[2048,2880]{0,1:T(8,128)(2,1)} async-done(((bf16[256,2880]{0,1:T(8,128)(2,1)}), bf16[2048,2880]{0,1:T(8,128)(2,1)}) %all-gather.5.cloned.1.call-update) | async-done | bytes 11796496 | tf_op jit(solution)/shard_map/all_gather | solution.py:87
  213.2 0.0 copy-done.3
  213.2 0.0 copy-start
  213.2 6.1 %multiply_reduce_fusion = (f32[128]{0:T(128)S(1)}, f32[128,2880]{0,1:T(8,128)S(1)}) fusion(bf16[2048,2880]{0,1:T(8,128)(2,1)} %all-gather.5.cloned.1.call-done, bf16[128,2048]{0,1:T(8,128)(2,1)S(1)} %bitcast.110, bf16[1,128,2880]{1,2,0:T(8,128)(2,1)S(1)} %copy-done.3), kind=kOutput, calls=%fused_computation.33 | convolution fusion | flops 1512161152 | bytes 14533120 | tf_op jit(solution)/shard_map/dot_general | solution.py:85
  219.4 0.0 copy-done
  219.4 4.0 convolution_convert_fusion
  223.4 8.5 %copy.38 = bf16[1024,2880]{1,0:T(8,128)(2,1)} copy(bf16[1024,2880]{0,1:T(8,128)(2,1)} %convolution_convert_fusion) | data formatting | bytes 11796480 | tf_op jit(solution)/shard_map/convert_element_type | solution.py:119
  231.9 10.1 %all-to-all-start = ((bf16[64,16,2880]{2,1,0:T(8,128)(2,1)}), bf16[64,16,2880]{2,1,0:T(8,128)(2,1)}, u32[]{:S(2)}, u32[]{:S(2)}) async-start(bf16[64,16,2880]{2,1,0:T(8,128)(2,1)} %bitcast.93), calls=%async_computation | async-start | bytes 12058624 | tf_op jit(solution)/shard_map/all_to_all | solution.py:120
  242.0 0.1 collective-permute-start
  242.1 0.5 collective-permute-start.1
  242.6 84.5 %all-to-all-done = bf16[64,16,2880]{2,1,0:T(8,128)(2,1)} async-done(((bf16[64,16,2880]{2,1,0:T(8,128)(2,1)}), bf16[64,16,2880]{2,1,0:T(8,128)(2,1)}, u32[]{:S(2)}, u32[]{:S(2)}) %all-to-all-start) | async-done | bytes 5898272 | tf_op jit(solution)/shard_map/all_to_all | solution.py:120
  327.1 13.5 %fusion.61 = f32[1024,1440]{0,1:T(8,128)S(1)} fusion(bf16[1024,2880]{1,0:T(8,128)(2,1)} %bitcast.22, bf16[1,2880,1440]{1,2,0:T(8,128)(2,1)} %param.20), kind=kOutput, calls=%fused_computation.89 | convolution fusion | flops 8493465600 | bytes 20090880 | tf_op jit(solution)/shard_map/dot_general | solution.py:125
  340.6 10.0 %fusion.19 = f32[1024,2880]{0,1:T(8,128)} fusion(f32[1024,1440]{0,1:T(8,128)S(1)} %fusion.61, bf16[1,720,2880]{2,1,0:T(8,128)(2,1)} %param.21), kind=kOutput, calls=%fused_computation.27 | convolution fusion | flops 4252631040 | bytes 21841920 | tf_op jit(solution)/shard_map/dot_general | solution.py:129
  350.7 0.0 collective-permute-done
  350.7 15.1 %fusion.72 = f32[1024,1440]{0,1:T(8,128)} fusion(bf16[1024,2880]{1,0:T(8,128)(2,1)} %bitcast.22, bf16[2880,1440]{0,1:T(8,128)(2,1)} %collective-permute-done), kind=kOutput, calls=%fused_computation.100 | convolution fusion | flops 8493465600 | bytes 20090880 | tf_op jit(solution)/shard_map/dot_general | solution.py:125
  365.8 0.0 collective-permute-done.1
  365.8 14.8 %add_convert_fusion = bf16[1024,2880]{0,1:T(8,128)(2,1)} fusion(f32[1024,2880]{0,1:T(8,128)} %fusion.19, bf16[720,2880]{1,0:T(8,128)(2,1)} %collective-permute-done.1, f32[1024,1440]{0,1:T(8,128)} %fusion.72), kind=kOutput, calls=%fused_computation.4 | convolution fusion | flops 4258529280 | bytes 27740160 | tf_op jit(solution)/shard_map/dot_general | solution.py:129
  380.6 8.5 %copy.39 = bf16[1024,2880]{1,0:T(8,128)(2,1)} copy(bf16[1024,2880]{0,1:T(8,128)(2,1)} %add_convert_fusion) | data formatting | bytes 11796480 | tf_op jit(solution)/shard_map/convert_element_type | solution.py:131
  389.1 0.0 copy-start.1
  389.1 0.0 copy-start.2
  389.1 11.1 %all-to-all-start.1 = ((bf16[64,16,2880]{2,1,0:T(8,128)(2,1)}), bf16[64,16,2880]{2,1,0:T(8,128)(2,1)}, u32[]{:S(2)}, u32[]{:S(2)}) async-start(bf16[64,16,2880]{2,1,0:T(8,128)(2,1)} %bitcast.94), calls=%async_computation.1 | async-start | bytes 12058624 | tf_op jit(solution)/shard_map/all_to_all | solution.py:132
  400.1 0.0 copy-done.1
  400.1 0.0 copy-done.2
  400.2 83.6 %all-to-all-done.1 = bf16[64,16,2880]{2,1,0:T(8,128)(2,1)} async-done(((bf16[64,16,2880]{2,1,0:T(8,128)(2,1)}), bf16[64,16,2880]{2,1,0:T(8,128)(2,1)}, u32[]{:S(2)}, u32[]{:S(2)}) %all-to-all-start.1) | async-done | bytes 5898272 | tf_op jit(solution)/shard_map/all_to_all | solution.py:132
  483.8 5.2 %convolution_bitcast_fusion = f32[128,2880]{0,1:T(8,128)S(1)} fusion(bf16[64,16,2880]{2,1,0:T(8,128)(2,1)} %all-to-all-done.1, f32[64,128]{1,0:T(8,128)S(1)} %bitcast.98, s32[64,128]{1,0:T(8,128)S(1)} %convolution_convert_fusion.1, pred[64,128]{1,0:T(8,128)(4,1)S(1)} %bitcast.101), kind=kOutput, calls=%fused_computation.11 | convolution fusion | flops 755892224 | bytes 7446528 | tf_op jit(solution)/shard_map/st,sd->td/dot_general | solution.py:135
  489.0 5.9 %fusion.10 = bf16[1,128,2880]{1,2,0:T(8,128)(2,1)} fusion(f32[128,2880]{0,1:T(8,128)S(1)} %get-tuple-element.8, f32[128,2880]{0,1:T(8,128)S(1)} %convolution_bitcast_fusion, bf16[64,16,2880]{2,1,0:T(8,128)(2,1)} %all-to-all-done.1, f32[64,128]{1,0:T(8,128)S(1)} %bitcast.99, s32[64,128]{1,0:T(8,128)S(1)} %convolution_convert_fusion.1, ...), kind=kOutput, calls=%fused_computation.16 | convolution fusion | flops 756473856 | bytes 9658368 | tf_op jit(solution)/shard_map/st,sd->td/dot_general | solution.py:135
  (7 shorter events, 0.1 us)
Async XLA Ops:
  6.5 50.4 %all-gather.3.cloned.1.call-start = ((), (), s32[]{:S(2)}) async-start(), calls=%async_computation.2 | async-start | bytes 1179648 | tf_op jit(solution)/shard_map/all_gather | solution.py:38
  8.1 205.1 %all-gather.5.cloned.1.call-start = ((), (), s32[]{:S(2)}) async-start(), calls=%async_computation.3 | async-start | bytes 13271040 | tf_op jit(solution)/shard_map/all_gather | solution.py:87
  67.9 145.3 %copy-start.3 = (bf16[1,128,2880]{1,2,0:T(8,128)(2,1)S(1)}, bf16[1,128,2880]{1,2,0:T(8,128)(2,1)}, u32[]{:S(2)}) copy-start(bf16[1,128,2880]{1,2,0:T(8,128)(2,1)} %param.14) | copy-start | bytes 2211844
  213.2 6.2 %copy-start = (f32[2880]{0:T(1024)S(1)}, f32[2880]{0:T(1024)}, u32[]{:S(2)}) copy-start(f32[2880]{0:T(1024)} %param.16) | copy-start | bytes 34564
  231.9 95.2 %all-to-all-start = ((bf16[64,16,2880]{2,1,0:T(8,128)(2,1)}), bf16[64,16,2880]{2,1,0:T(8,128)(2,1)}, u32[]{:S(2)}, u32[]{:S(2)}) async-start(bf16[64,16,2880]{2,1,0:T(8,128)(2,1)} %bitcast.93), calls=%async_computation | async-start | bytes 12058624 | tf_op jit(solution)/shard_map/all_to_all | solution.py:120
  242.0 108.7 %collective-permute-start = (bf16[2880,1440]{0,1:T(8,128)(2,1)}, bf16[2880,1440]{0,1:T(8,128)(2,1)}, u32[]{:S(2)}, u32[]{:S(2)}) collective-permute-start(bf16[2880,1440]{0,1:T(8,128)(2,1)} %bitcast.108), channel_id=1, source_target_pairs={{0,1},{1,0},{2,3},{3,2},{4,5},{5,4},{6,7},{7,6},{8,9},{9,8},{10,11... | collective-permute-start | bytes 24883208 | tf_op jit(solution)/shard_map/ppermute | solution.py:81
  242.1 123.7 %collective-permute-start.1 = (bf16[720,2880]{1,0:T(8,128)(2,1)}, bf16[720,2880]{1,0:T(8,128)(2,1)}, u32[]{:S(2)}, u32[]{:S(2)}) collective-permute-start(bf16[720,2880]{1,0:T(8,128)(2,1)} %bitcast.109), channel_id=1, source_target_pairs={{0,1},{1,0},{2,3},{3,2},{4,5},{5,4},{6,7},{7,6},{8,9},{9,8},{10,11... | collective-permute-start | bytes 12441608 | tf_op jit(solution)/shard_map/ppermute | solution.py:82
  389.1 11.1 %copy-start.1 = (s32[1,128,4]{1,2,0:T(4,128)S(1)}, s32[1,128,4]{1,2,0:T(4,128)}, u32[]{:S(2)}) copy-start(s32[1,128,4]{1,2,0:T(4,128)} %param.18) | copy-start | bytes 6148
  389.1 11.1 %copy-start.2 = (f32[1,128,4]{1,2,0:T(4,128)S(1)}, f32[1,128,4]{1,2,0:T(4,128)}, u32[]{:S(2)}) copy-start(f32[1,128,4]{1,2,0:T(4,128)} %param.19) | copy-start | bytes 6148
  389.1 94.7 %all-to-all-start.1 = ((bf16[64,16,2880]{2,1,0:T(8,128)(2,1)}), bf16[64,16,2880]{2,1,0:T(8,128)(2,1)}, u32[]{:S(2)}, u32[]{:S(2)}) async-start(bf16[64,16,2880]{2,1,0:T(8,128)(2,1)} %bitcast.94), calls=%async_computation.1 | async-start | bytes 12058624 | tf_op jit(solution)/shard_map/all_to_all | solution.py:132
Sparse Core Ops, SparseCore 0:
  9.7 47.1 all-gather.2
  59.1 154.0 all-gather.4

commit v2 on v1

v2 whole, which is shorter than its diff:
```python
import functools
import jax
import jax.numpy as jnp
from jax import lax
from jax.experimental import pallas as pl
from jax.experimental.pallas import tpu as pltpu
from jax.sharding import Mesh, PartitionSpec as P

D = 2880
HALF_D = D // 2
HEAD = 64
TOK = 128
QUARTER = 224
REST = HALF_D - 4 * QUARTER
AXES = ("y_hi", "x", "y_lo", "z", "core")
MESH = pl.DeviceIdType.MESH


def here():
    return {a: lax.axis_index(a) for a in AXES}


def moved(me, axis, by):
    to = dict(me)
    if axis == "y":
        y = (me["y_hi"] * 2 + me["y_lo"] + by) % 4
        to["y_hi"], to["y_lo"] = y // 2, y % 2
    else:
        to[axis] = (me[axis] + by) % 4
    return to


class Copies:
    def __init__(self, send, recv):
        self.send, self.recv, self.made = send, recv, []

    def go(self, src, dst, to):
        i = len(self.made)
        c = pltpu.make_async_remote_copy(
            src_ref=src, dst_ref=dst, send_sem=self.send.at[i], recv_sem=self.recv.at[i],
            device_id=to, device_id_type=MESH,
        )
        c.start()
        self.made.append(c)
        return c

    def drain(self):
        for c in self.made:
            c.wait_send()


def greet(peers):
    barrier = pltpu.get_barrier_semaphore()
    for peer in peers:
        pl.semaphore_signal(barrier, inc=1, device_id=peer, device_id_type=MESH)
    pl.semaphore_wait(barrier, len(peers))


FRONT_COPIES = 80


def front_kernel(
    order, q, k, v, hid, gain, ow, gu, dn,
    residual, moe_in, gu_oth, dn_oth,
    kv, w, att, acc, got, send, recv, local_sem,
):
    me = here()
    cp = Copies(send, recv)
    core = me["core"]
    other = dict(me, core=1 - core)
    kv_mate = dict(me, y_hi=1 - me["y_hi"])
    w_mate = dict(me, y_hi=1 - me["y_hi"], y_lo=1 - me["y_lo"])
    xp, xm = moved(me, "x", 1), moved(me, "x", 3)
    zp, zm = moved(me, "z", 1), moved(me, "z", 3)
    z = me["z"]
    base = pl.multiple_of(core * HALF_D, 16)
    greet([other, kv_mate, w_mate, xp, xm, zp, zm])

    def quarter(t, part=None):
        start = REST + QUARTER * ((z + t) % 4)
        size = QUARTER
        if part is not None:
            size = QUARTER // 2
            start = start + part * size
        return pl.ds(pl.multiple_of(start, 16), size)

    own_q = ow.at[pl.ds(pl.multiple_of(base + REST + QUARTER * z, 16), QUARTER)]
    own_r = ow.at[pl.ds(base, REST)]
    rest = pl.ds(0, REST)
    rest_parts = (pl.ds(0, REST // 2), pl.ds(REST // 2, REST // 2))

    own_w = pltpu.make_async_copy(ow.at[pl.ds(base, HALF_D)], w.at[0], local_sem.at[0])
    own_w.start()
    kv[0, :, pl.ds(0, 256)] = k[...]
    kv[0, :, pl.ds(256, 256)] = v[...]

    yq = cp.go(own_q, w.at[4, quarter(0)], w_mate)
    xq = {0: (cp.go(own_q, w.at[3, quarter(0)], xp), cp.go(own_q, w.at[1, quarter(0)], xm))}
    ky = cp.go(kv.at[0], kv.at[4], kv_mate)
    kx = {0: (cp.go(kv.at[0], kv.at[3], xp), cp.go(kv.at[0], kv.at[1], xm))}
    yr = cp.go(own_r, w.at[4, rest], w_mate)
    xr = {0: (cp.go(own_r, w.at[3, rest], xp), cp.go(own_r, w.at[1, rest], xm))}
    swaps = [cp.go(gu, gu_oth, other), cp.go(dn, dn_oth, other)]
    zq, zq2 = {}, {}

    def z_first(slot):
        rows = quarter(0)
        zq[slot] = (
            cp.go(w.at[slot, rows], w.at[slot, rows], zp),
            cp.go(w.at[slot, rows], w.at[slot, rows], zm),
        )

    def z_second(slot):
        zq[slot][0].wait_recv()
        a = w.at[slot, quarter(3, 0)]
        zq[slot][1].wait_recv()
        b = w.at[slot, quarter(1, 1)]
        zq2[slot] = (cp.go(a, a, zp), cp.go(b, b, zm))

    def x_second(buf, d, firsts, parts):
        for c in firsts:
            c.wait_recv()
        return (
            cp.go(buf.at[4 * d + 3, parts[0]], buf.at[4 * d + 2, parts[0]], xp),
            cp.go(buf.at[4 * d + 1, parts[1]], buf.at[4 * d + 2, parts[1]], xm),
        )

    kv_parts = (pl.ds(0, 64), pl.ds(64, 64))
    q_parts = (quarter(0, 0), quarter(0, 1))
    yq.wait_recv()
    xq[1] = (
        cp.go(w.at[4, quarter(0)], w.at[7, quarter(0)], xp),
        cp.go(w.at[4, quarter(0)], w.at[5, quarter(0)], xm),
    )
    z_first(4)
    x2q = {0: x_second(w, 0, xq[0], q_parts)}
    z_first(3)
    z_first(1)
    ky.wait_recv()
    kx[1] = (cp.go(kv.at[4], kv.at[7], xp), cp.go(kv.at[4], kv.at[5], xm))
    kx2 = {0: x_second(kv, 0, kx[0], kv_parts)}
    x2q[1] = x_second(w, 1, xq[1], q_parts)
    z_first(7)
    z_first(5)
    kx2[1] = x_second(kv, 1, kx[1], kv_parts)
    for c in x2q[0]:
        c.wait_recv()
    z_first(2)
    for c in x2q[1]:
        c.wait_recv()
    z_first(6)
    z_second(4)
    yr.wait_recv()
    xr[1] = (cp.go(w.at[4, rest], w.at[7, rest], xp), cp.go(w.at[4, rest], w.at[5, rest], xm))
    for d in (0, 1):
        for c in kx2[d]:
            c.wait_recv()

    ctx = me["y_hi"] * 4 + me["x"]
    col = lax.broadcasted_iota(jnp.int32, (1, 1024), 1)
    key_pos = col % 64
    for slot in range(8):
        block = ((me["y_hi"] + slot // 4) % 2) * 4 + (me["x"] + slot % 4) % 4
        for h in (0, 1):
            key_pos = key_pos + jnp.where(
                col // 64 == 2 * slot + h, order[2 * block + h] * 64, 0
            )
    row = lax.broadcasted_iota(jnp.int32, (256, 1), 0) % TOK
    query_pos = row % 64 + jnp.where(row < 64, order[2 * ctx] * 64, order[2 * ctx + 1] * 64)
    bias = jnp.where(key_pos <= query_pos, 0.0, -1e30)

    def group(g):
        keys = kv[:, :, 64 * g : 64 * g + 64].reshape(1024, HEAD)
        values = kv[:, :, 256 + 64 * g : 256 + 64 * g + 64].reshape(1024, HEAD)

        def pair(i, _):
            lanes = pl.ds(pl.multiple_of((4 * g + i) * 128, 128), 128)
            two = q[:, lanes] * jnp.bfloat16(0.125)
            two = jnp.concatenate([two[:, :HEAD], two[:, HEAD:]], axis=0)
            s = lax.dot_general(
                two, keys, (((1,), (1,)), ((), ())), preferred_element_type=jnp.float32
            ) + bias
            p = jnp.exp(s - jnp.max(s, axis=1, keepdims=True))
            total = jnp.sum(p, axis=1, keepdims=True)
            o = jnp.dot(p.astype(jnp.bfloat16), values, preferred_element_type=jnp.float32)
            o = (o / total).astype(jnp.bfloat16)
            att[0, :, lanes] = jnp.concatenate([o[:TOK], o[TOK:]], axis=1)
            return 0

        lax.fori_loop(0, 4, pair, 0)

    group(0)
    z_second(3)
    z_second(1)
    x2r = {0: x_second(w, 0, xr[0], rest_parts)}
    group(1)
    z_second(7)
    z_second(5)
    group(2)
    x2r[1] = x_second(w, 1, xr[1], rest_parts)
    z_second(2)
    z_second(6)
    group(3)
    att_out = cp.go(att.at[0], att.at[1], other)
    own_w.wait()
    att_out.wait_recv()

    def project(slot, first=False):
        block = ((me["y_hi"] + slot // 4) % 2) * 4 + (me["x"] + slot % 4) % 4
        lanes = pl.ds(pl.multiple_of(block * 256, 256), 256)
        both = att[:, :, lanes].reshape(2 * TOK, 256)
        part = lax.dot_general(
            both, w[slot], (((1,), (1,)), ((), ())), preferred_element_type=jnp.float32
        ).reshape(2, TOK, HALF_D)
        acc[...] = part if first else acc[...] + part

    project(0, True)
    for slot in (4, 3, 1, 7, 5, 2, 6):
        d, s = slot // 4, slot % 4
        if slot == 4:
            pass
        elif s == 2:
            for c in x2r[d]:
                c.wait_recv()
        for c in zq2[slot]:
            c.wait_recv()
        project(slot)
    back = cp.go(acc.at[1], got, other)
    hidden = hid[...].astype(jnp.float32)
    back.wait_recv()
    mine, theirs = acc[0], got[...]
    left = jnp.where(core == 0, mine, theirs)
    right = jnp.where(core == 0, theirs, mine)
    res = (hidden + jnp.concatenate([left, right], axis=1)).astype(jnp.bfloat16)
    residual[...] = res
    res = res.astype(jnp.float32)
    scale = lax.rsqrt(jnp.mean(res * res, axis=1, keepdims=True) + 1e-05)
    moe_in[...] = (res * scale * gain[...]).astype(jnp.bfloat16)
    for c in swaps:
        c.wait_recv()
    cp.drain()


def front(q, k, v, hidden, gain, ow_t, order, gu_t, dn):
    vmem, anyspace = pl.BlockSpec(memory_space=pltpu.VMEM), pl.BlockSpec(memory_space=pl.ANY)
    bf = jnp.bfloat16
    return pl.pallas_call(
        front_kernel,
        out_shape=(
            jax.ShapeDtypeStruct((TOK, D), bf), jax.ShapeDtypeStruct((TOK, D), bf),
            jax.ShapeDtypeStruct(gu_t.shape, bf), jax.ShapeDtypeStruct(dn.shape, bf),
        ),
        in_specs=[pl.BlockSpec(memory_space=pltpu.SMEM), vmem, vmem, vmem, vmem, vmem, anyspace, anyspace, anyspace],
        out_specs=(vmem, vmem, anyspace, anyspace),
        scratch_shapes=[
            pltpu.VMEM((8, TOK, 512), bf),
            pltpu.VMEM((8, HALF_D, 256), bf),
            pltpu.VMEM((2, TOK, 2048), bf),
            pltpu.VMEM((2, TOK, HALF_D), jnp.float32),
            pltpu.VMEM((TOK, HALF_D), jnp.float32),
            pltpu.SemaphoreType.DMA((FRONT_COPIES,)),
            pltpu.SemaphoreType.DMA((FRONT_COPIES,)),
            pltpu.SemaphoreType.DMA((1,)),
        ],
        compiler_params=pltpu.CompilerParams(
            collective_id=0, has_side_effects=True, vmem_limit_bytes=48 * 2**20
        ),
    )(order, q, k, v, hidden, gain, ow_t, gu_t, dn)


TOPK = 4
EXPERTS = 64
CAP = 16

CTX = ("y_hi", "x")
EXP = ("y_lo", "z", "core")
CHIPS = ("y_hi", "x", "y_lo", "z")


def local(
    queries,
    key_rows,
    value_matrix,
    hidden,
    out_weight,
    norm_gain,
    block_order,
    expert_ids,
    route_weights,
    gate_up_weight,
    down_weight,
):
    gate_up_own, down_own = gate_up_weight[0].T, down_weight[0]
    residual, moe_in, gate_up_oth, down_oth = front(
        queries[0], key_rows[0], value_matrix[0], hidden[0], norm_gain[None], out_weight.T,
        block_order, gate_up_own, down_own,
    )
    gate_up_own, gate_up_oth = gate_up_own.T, gate_up_oth.T
    res_float = residual.astype(jnp.float32)

    ids, weights = expert_ids[0], route_weights[0]
    token_count = ids.shape[0]
    named = ids[:, :, None] == jnp.arange(EXPERTS, dtype=jnp.int32)
    member = jnp.any(named, axis=1)
    weight_of = jnp.sum(jnp.where(named, weights[:, :, None], 0.0), axis=1)
    tok = jnp.arange(token_count, dtype=jnp.int32)
    before = (tok[None, :] < tok[:, None]).astype(jnp.bfloat16)
    slot = jnp.dot(
        before, member.astype(jnp.bfloat16), preferred_element_type=jnp.float32
    ).astype(jnp.int32)
    place = (
        member.T[:, None, :]
        & (slot.T[:, None, :] == jnp.arange(CAP, dtype=jnp.int32)[None, :, None])
    ).reshape(EXPERTS * CAP, token_count)
    picked = place.astype(jnp.bfloat16)
    spread = jnp.where(
        place, jnp.broadcast_to(weight_of.T[:, None, :], (EXPERTS, CAP, token_count)).reshape(EXPERTS * CAP, token_count), 0.0
    )
    high = spread.astype(jnp.bfloat16)
    low = (spread - high.astype(jnp.float32)).astype(jnp.bfloat16)

    outgoing = jnp.dot(picked, moe_in, preferred_element_type=jnp.float32).astype(jnp.bfloat16)
    rows = lax.all_to_all(
        outgoing.reshape(EXPERTS, CAP, D), CHIPS, split_axis=0, concat_axis=0, tiled=True
    ).reshape(EXPERTS * CAP, D)

    def half(gate_up, down):
        gate_up_out = jnp.dot(rows, gate_up, preferred_element_type=jnp.float32)
        n = gate_up.shape[1] // 2
        gate, up = gate_up_out[:, :n], gate_up_out[:, n:]
        act = (gate * jax.nn.sigmoid(1.702 * gate) * (up + 1.0)).astype(jnp.bfloat16)
        return jnp.dot(act, down, preferred_element_type=jnp.float32)

    result = (half(gate_up_own, down_own) + half(gate_up_oth, down_oth)).astype(jnp.bfloat16)
    returned = lax.all_to_all(
        result.reshape(EXPERTS, CAP, D), CHIPS, split_axis=0, concat_axis=0, tiled=True
    ).reshape(EXPERTS * CAP, D)
    mixed = jnp.einsum("st,sd->td", high, returned, preferred_element_type=jnp.float32) + jnp.einsum(
        "st,sd->td", low, returned, preferred_element_type=jnp.float32
    )
    return (res_float + mixed).astype(jnp.bfloat16)[None]


def solution(mesh):
    fine = Mesh(mesh.devices.reshape(2, 4, 2, 4, 2), ("y_hi", "x", "y_lo", "z", "core"))
    rows = P(EXP, CTX, None)
    halves = P(CTX + EXP, None, None)
    return jax.shard_map(
        local,
        mesh=fine,
        in_specs=(
            rows, rows, rows, rows, P(CTX, None), P(), P(), rows, rows, halves, halves,
        ),
        out_specs=rows,
        check_vma=False,
    )
```

time: 510 us -> 317 us (0.62)
  waiting for transfers between devices: 352 us -> 86.3 us
  blocking collectives: 0 us -> 80.5 us
  Pallas kernels: 0 us -> 50.4 us
  matrix products: 90.5 us -> 57.7 us
  between operations: 13.6 us -> 0.15 us
  starting transfers between devices: 21.8 us -> 9.51 us
  local copies, waits for them, and re-layouts: 19.9 us -> 25 us
    all_gather x2 -> x0, waiting for transfers between devices: 183 us -> none  [the longest x1 139 us: local(): lax.all_gather(out_weight, CTX, axis=0, tiled=True)]
    all_to_all x1 -> x0, waiting for transfers between devices: 84.5 us -> none  [local(): lax.all_to_all(outgoing.reshape(EXPERTS, CAP, D), CHIPS, split_axis=0, co...]
    all_to_all x0 -> x1, blocking collectives: none -> 80.5 us  [local(): lax.all_to_all(outgoing.reshape(EXPERTS, CAP, D), CHIPS, split_axis=0, co...]
    pallas_call x0 -> x1, Pallas kernels: none -> 50.4 us  [front(): pl.pallas_call(front_kernel, out_shape=(jax.ShapeDtypeStruct((TOK, D), bf...]
    dot_general x2 -> x0, matrix products: 12.2 us -> none  [the longest x1 6.14 us: local(): jnp.dot(attended, lax.all_gather(out_weight, CTX, axis=0, tiled=True), pr...]
    all_to_all x1 -> x0, starting transfers between devices: 10.1 us -> none  [local(): lax.all_to_all(outgoing.reshape(EXPERTS, CAP, D), CHIPS, split_axis=0, co...]
    sub x1 -> x0, matrix products: 9.53 us -> none  [attention(): kept_probs = jnp.where(visible, jnp.exp(masked - new_max[..., None]), 0.0)]
    dot_general x2, matrix products: 28.7 us -> 23.1 us  [half(): gate_up_out = jnp.dot(rows, gate_up, preferred_element_type=jnp.float32)]
  transfers between devices with their start and end apart: 6 -> 1, of which waited for: 4 -> 1; matrix products, arithmetic and copies ran while one was open for 12% -> 0% of each run, Pallas kernels for 0% -> 0%
where the time goes in v2:
time: 317 us; the launch traced here: 311 us
  waiting for transfers between devices  86.3 us (27%)
  blocking collectives  80.5 us (25%)
  matrix products  57.7 us (18%)
  Pallas kernels  50.4 us (16%)
  local copies, waits for them, and re-layouts  25 us (8%)
  starting transfers between devices  9.51 us (3%)
    all_to_all x1, waiting for transfers between devices, local(): lax.all_to_all(result.reshape(EXPERTS, CAP, D), CHIPS, split_axis=0, conc...  86.3 us
    all_to_all x1, blocking collectives, local(): lax.all_to_all(outgoing.reshape(EXPERTS, CAP, D), CHIPS, split_axis=0, co...  80.5 us
    pallas_call x1, Pallas kernels, front(): pl.pallas_call(front_kernel, out_shape=(jax.ShapeDtypeStruct((TOK, D), bf...  50.4 us
    dot_general x2, matrix products, half(): gate_up_out = jnp.dot(rows, gate_up, preferred_element_type=jnp.float32)  23.1 us
    dot_general x2, matrix products, half(): return jnp.dot(act, down, preferred_element_type=jnp.float32)  22.8 us
    all_to_all x1, starting transfers between devices, local(): lax.all_to_all(result.reshape(EXPERTS, CAP, D), CHIPS, split_axis=0, conc...  9.51 us
    convert_element_type x1, local copies, waits for them, and re-layouts, local(): (half(gate_up_own, down_own) + half(gate_up_oth, down_oth)).astype(jnp.bf...  8.51 us
    convert_element_type x1, local copies, waits for them, and re-layouts, local(): jnp.dot(picked, moe_in, preferred_element_type=jnp.float32)  8.29 us
  transfers between devices with their start and end apart: 1, of which 1 were waited for; matrix products, arithmetic and copies ran while one was open for 0% of the time, Pallas kernels for 0%

profile of v2, /device:TPU:58, one launch (start us, length us, event | category | flops | bytes accessed | tf_op | source)
XLA Modules:
  0.0 310.5 jit_solution(5777759406542040985)
XLA Ops:
  0.0 0.7 fusion.29
  0.7 0.1 convolution_convert_fusion.1
  0.9 0.1 eq.50
  0.9 1.5 copy.38
  2.4 0.7 broadcast_in_dim.36.gain
  3.1 0.2 fusion.19
  3.3 0.0 copy-start
  3.3 1.4 copy-done
  4.7 0.0 copy-start.1
  4.7 1.0 copy-done.1
  5.8 0.0 copy-start.2
  5.8 0.8 copy-done.2
  6.6 0.0 copy-start.3
  6.6 0.8 copy-done.3
  7.4 0.0 copy-start.4
  7.4 0.7 copy-done.4
  8.1 50.4 %shard_map.109 = (bf16[128,2880]{1,0:T(8,128)(2,1)S(1)}, bf16[128,2880]{1,0:T(8,128)(2,1)S(1)}, bf16[1440,2880]{1,0:T(8,128)(2,1)}, bf16[720,2880]{1,0:T(8,128)(2,1)}) custom-call(s32[16]{0:T(128)S(1)} %copy-done.4, bf16[128,2048]{1,0:T(8,128)(2,1)S(1)} %bitcast.51, bf16[128,256]{1,0:T(8,128)(2,1)S(1)} %bitcast.52, bf16[128,256]{1,0:T(8,128)(2,1)S(1)} %bitcast.53, ...), custom_call_target="tpu_custom_call" | custom-call | tf_op jit(solution)/shard_map/pallas_call | solution.py:247
  58.5 4.2 %convolution_convert_fusion = bf16[1024,2880]{0,1:T(8,128)(2,1)} fusion(pred[1024,128]{1,0:T(32,128)(4,1)S(1)} %fusion.19, bf16[128,2880]{1,0:T(8,128)(2,1)S(1)} %get-tuple-element.10), kind=kOutput, calls=%fused_computation.3 | convolution fusion | flops 757923840 | bytes 6766592 | tf_op jit(solution)/shard_map/dot_general | solution.py:322
  62.7 8.3 %copy.39 = bf16[1024,2880]{1,0:T(8,128)(2,1)} copy(bf16[1024,2880]{0,1:T(8,128)(2,1)} %convolution_convert_fusion) | data formatting | bytes 11796480 | tf_op jit(solution)/shard_map/convert_element_type | solution.py:322
  71.0 0.0 slice-start.2
  71.0 80.5 %all_to_all.10 = bf16[64,16,2880]{2,1,0:T(8,128)(2,1)S(1)} all-to-all(bf16[64,16,2880]{2,1,0:T(8,128)(2,1)} %bitcast.55), channel_id=1, replica_groups=mesh['y_hi'=2,'x'=4,'y_lo'=2,'z'=4,'core'=2] {'y_hi','x','y_lo','z'}, dimensions={0} | all-to-all | bytes 11796480 | tf_op jit(solution)/shard_map/all_to_all | solution.py:323
  151.6 0.0 slice-start.3
  151.6 0.0 slice-start.4
  151.6 0.0 slice-start
  151.6 11.9 %fusion = f32[1024,1440]{0,1:T(8,128)S(1)} fusion(bf16[1024,2880]{1,0:T(8,128)(2,1)S(1)} %bitcast.57, bf16[1,2880,1440]{1,2,0:T(8,128)(2,1)} %param.20), kind=kOutput, calls=%fused_computation.1 | convolution fusion | flops 8493465600 | bytes 20090880 | tf_op jit(solution)/shard_map/dot_general | solution.py:328
  163.5 0.0 slice-start.1
  163.5 0.0 slice-done.2
  163.5 0.0 slice-done.3
  163.5 0.0 slice-done.4
  163.5 11.2 %fusion.37 = f32[1024,1440]{0,1:T(8,128)} fusion(bf16[1024,2880]{1,0:T(8,128)(2,1)S(1)} %bitcast.58, bf16[1440,2880]{1,0:T(8,128)(2,1)S(1)} %bitcast.71), kind=kOutput, calls=%fused_computation.48 | convolution fusion | flops 8493465600 | bytes 20090880 | tf_op jit(solution)/shard_map/dot_general | solution.py:328
  174.7 0.0 slice-done
  174.7 0.0 slice-done.1
  174.7 7.9 %fusion.10 = f32[1024,2880]{0,1:T(8,128)} fusion(f32[1024,1440]{0,1:T(8,128)S(1)} %fusion, bf16[1,720,2880]{2,1,0:T(8,128)(2,1)S(1)} %bitcast.61), kind=kOutput, calls=%fused_computation.16 | convolution fusion | flops 4252631040 | bytes 21841920 | tf_op jit(solution)/shard_map/dot_general | solution.py:332
  182.5 14.9 %add_convert_fusion = bf16[1024,2880]{0,1:T(8,128)(2,1)} fusion(f32[1024,2880]{0,1:T(8,128)} %fusion.10, bf16[720,2880]{1,0:T(8,128)(2,1)} %get-tuple-element.12, f32[1024,1440]{0,1:T(8,128)} %fusion.37), kind=kOutput, calls=%fused_computation | convolution fusion | flops 4258529280 | bytes 27740160 | tf_op jit(solution)/shard_map/dot_general | solution.py:332
  197.5 8.5 %copy.40 = bf16[1024,2880]{1,0:T(8,128)(2,1)} copy(bf16[1024,2880]{0,1:T(8,128)(2,1)} %add_convert_fusion) | data formatting | bytes 11796480 | tf_op jit(solution)/shard_map/convert_element_type | solution.py:334
  206.0 0.0 copy-start.5
  206.0 0.0 copy-start.6
  206.0 9.5 %all-to-all-start.1 = ((bf16[64,16,2880]{2,1,0:T(8,128)(2,1)}), bf16[64,16,2880]{2,1,0:T(8,128)(2,1)}, u32[]{:S(2)}, u32[]{:S(2)}) async-start(bf16[64,16,2880]{2,1,0:T(8,128)(2,1)} %bitcast.54), calls=%async_computation.1 | async-start | bytes 12058624 | tf_op jit(solution)/shard_map/all_to_all | solution.py:335
  215.5 0.0 copy-done.5
  215.5 0.0 copy-done.6
  215.5 86.3 %all-to-all-done.1 = bf16[64,16,2880]{2,1,0:T(8,128)(2,1)} async-done(((bf16[64,16,2880]{2,1,0:T(8,128)(2,1)}), bf16[64,16,2880]{2,1,0:T(8,128)(2,1)}, u32[]{:S(2)}, u32[]{:S(2)}) %all-to-all-start.1) | async-done | bytes 5898272 | tf_op jit(solution)/shard_map/all_to_all | solution.py:335
  301.8 3.8 %convolution_bitcast_fusion = f32[128,2880]{1,0:T(8,128)S(1)} fusion(bf16[64,16,2880]{2,1,0:T(8,128)(2,1)} %all-to-all-done.1, f32[64,128]{1,0:T(8,128)S(1)} %bitcast.62, s32[64,128]{1,0:T(8,128)S(1)} %convolution_convert_fusion.1, pred[64,128]{1,0:T(8,128)(4,1)S(1)} %bitcast.65), kind=kOutput, calls=%fused_computation.4 | convolution fusion | flops 755892224 | bytes 7446528 | tf_op jit(solution)/shard_map/st,sd->td/dot_general | solution.py:338
  305.6 3.8 %fusion.5 = bf16[1,128,2880]{2,1,0:T(8,128)(2,1)S(1)} fusion(f32[128,2880]{1,0:T(8,128)S(1)} %convolution_bitcast_fusion, bf16[64,16,2880]{2,1,0:T(8,128)(2,1)} %all-to-all-done.1, bf16[128,2880]{1,0:T(8,128)(2,1)S(1)} %get-tuple-element.9, f32[64,128]{1,0:T(8,128)S(1)} %bitcast.63, s32[64,128]{1,0:T(8,128)S(1)} %convolution_convert_fusion.1, ...), kind=kOutput, calls=%fused_computation.9 | convolution fusion | flops 756842496 | bytes 8921088 | tf_op jit(solution)/shard_map/st,sd->td/dot_general | solution.py:338
  309.4 1.1 copy.43
  (4 shorter events, 0.0 us)
Async XLA Ops:
  3.3 1.4 copy-start
  4.7 1.0 copy-start.1
  5.8 0.8 copy-start.2
  6.6 0.8 copy-start.3
  7.4 0.7 copy-start.4
  71.0 92.5 %slice-start.2 = ((s8[8478720]{0:T(1024)(128)(4,1)}), s8[4194304]{0:T(1024)(128)(4,1)S(1)}, s32[]{:S(2)}) async-start(s8[8478720]{0:T(1024)(128)(4,1)} %bitcast.70), calls=%async_computation.4 | async-start | bytes 8388608
  151.6 11.9 %slice-start.3 = ((s8[8478720]{0:T(1024)(128)(4,1)}), s8[4194304]{0:T(1024)(128)(4,1)S(1)}, s32[]{:S(2)}) async-start(s8[8478720]{0:T(1024)(128)(4,1)} %bitcast.70), calls=%async_computation.5 | async-start | bytes 8388608
  151.6 11.9 %slice-start.4 = ((s8[8478720]{0:T(1024)(128)(4,1)}), s8[90112]{0:T(1024)(128)(4,1)S(1)}, s32[]{:S(2)}) async-start(s8[8478720]{0:T(1024)(128)(4,1)} %bitcast.70), calls=%async_computation.6 | async-start | bytes 180224
  151.6 23.1 %slice-start = ((s8[4239360]{0:T(1024)(128)(4,1)}), s8[4194304]{0:T(1024)(128)(4,1)S(1)}, s32[]{:S(2)}) async-start(s8[4239360]{0:T(1024)(128)(4,1)} %bitcast.60), calls=%async_computation.2 | async-start | bytes 8388608
  163.5 11.2 %slice-start.1 = ((s8[4239360]{0:T(1024)(128)(4,1)}), s8[45056]{0:T(1024)(128)(4,1)S(1)}, s32[]{:S(2)}) async-start(s8[4239360]{0:T(1024)(128)(4,1)} %bitcast.60), calls=%async_computation.3 | async-start | bytes 90112
  206.0 9.5 %copy-start.5 = (s32[1,128,4]{1,2,0:T(4,128)S(1)}, s32[1,128,4]{1,2,0:T(4,128)}, u32[]{:S(2)}) copy-start(s32[1,128,4]{1,2,0:T(4,128)} %param.18) | copy-start | bytes 6148
  206.0 9.5 %copy-start.6 = (f32[1,128,4]{1,2,0:T(4,128)S(1)}, f32[1,128,4]{1,2,0:T(4,128)}, u32[]{:S(2)}) copy-start(f32[1,128,4]{1,2,0:T(4,128)} %param.19) | copy-start | bytes 6148
  206.0 95.8 %all-to-all-start.1 = ((bf16[64,16,2880]{2,1,0:T(8,128)(2,1)}), bf16[64,16,2880]{2,1,0:T(8,128)(2,1)}, u32[]{:S(2)}, u32[]{:S(2)}) async-start(bf16[64,16,2880]{2,1,0:T(8,128)(2,1)} %bitcast.54), calls=%async_computation.1 | async-start | bytes 12058624 | tf_op jit(solution)/shard_map/all_to_all | solution.py:335

commit v3 on v2

--- a/solution.py
+++ b/solution.py
@@ -14,6 +14,8 @@
 REST = HALF_D - 4 * QUARTER
 AXES = ("y_hi", "x", "y_lo", "z", "core")
 MESH = pl.DeviceIdType.MESH
+CTX = ("y_hi", "x")
+EXP = ("y_lo", "z", "core")
 
 
 def here():
@@ -268,77 +270,312 @@
     )(order, q, k, v, hidden, gain, ow_t, gu_t, dn)
 
 
-TOPK = 4
-EXPERTS = 64
-CAP = 16
-
-CTX = ("y_hi", "x")
-EXP = ("y_lo", "z", "core")
-CHIPS = ("y_hi", "x", "y_lo", "z")
+PIECES = ((0, 1024), (1024, 1024), (2048, 832))
+TURNS = (("x", "y", "z"), ("y", "z", "x"), ("z", "x", "y"))
+ORDER = (0, 2, 1, 3)
+MOE_COPIES = 200
+STEP = 240
+
+
+def moe_kernel(
+    table, moe_in, residual, gu0, gu1, dn0, dn1,
+    out, *refs,
+):
+    r2, q3, q2 = refs[0:3], refs[3:6], refs[6:9]
+    t, s_buf, r3, tab, part, got = (refs[9 + 3 * i : 12 + 3 * i] for i in range(6))
+    gu, dn, ffn, acc, send, recv, local_sem = refs[27:]
+    me = here()
+    cp = Copies(send, recv)
+    near = []
+
+    def copy(src, dst):
+        c = pltpu.make_async_copy(src, dst, local_sem.at[len(near)])
+        c.start()
+        near.append(c)
+        return c
+
+    def go(src, dst, axis, by):
+        if by == 0:
+            return copy(src, dst)
+        return cp.go(src, dst, moved(me, axis, by))
+
+    def arrive(cs):
+        for c in cs:
+            if any(c is n for n in near):
+                c.wait()
+            else:
+                c.wait_recv()
+
+    greet([moved(me, a, by) for a in ("x", "y", "z") for by in (1, 3, 2)])
+    loads = [copy(gu0, gu.at[0]), copy(gu1, gu.at[1]), copy(dn0, dn.at[0]), copy(dn1, dn.at[1])]
+
+    tabs, ones, twos = {}, {}, {}
+    for p in range(3):
+        tab[p][0] = table[...]
+        lo, width = PIECES[p]
+        t[p][0] = moe_in[:, lo : lo + width]
+    for p in range(3):
+        a = TURNS[p][0]
+        tabs[p] = [go(tab[p].at[0], tab[p].at[4 - by], a, by) for by in (1, 3, 2)]
+    for p in range(3):
+        a = TURNS[p][0]
+        ones[p] = {3: go(t[p].at[0], t[p].at[3], a, 1), 1: go(t[p].at[0], t[p].at[1], a, 3)}
+    halves = (pl.ds(0, 64), pl.ds(64, 64))
+    for p in range(3):
+        a = TURNS[p][0]
+        ones[p][3].wait_recv()
+        x = go(t[p].at[3, halves[0]], t[p].at[2, halves[0]], a, 1)
+        ones[p][1].wait_recv()
+        twos[p] = [x, go(t[p].at[1, halves[1]], t[p].at[2, halves[1]], a, 3)]
+
+    row = lax.broadcasted_iota(jnp.int32, (256, 1), 0)
+    y_me = me["y_hi"] * 2 + me["y_lo"]
+
+    def row_code(p):
+        at = {"x": me["x"], "y": y_me, "z": me["z"]}
+        _, b, c = TURNS[p]
+        at[b] = (at[b] + row // 64) % 4
+        at[c] = (at[c] + (row // 16) % 4) % 4
+        expert = (at["y"] // 2) * 32 + at["x"] * 8 + (at["y"] % 2) * 4 + at["z"]
+        return (expert * 16 + row % 16).astype(jnp.float32)
+
+    def rows_of(p, s):
+        return s_buf[p].at[:, :, s] if p < 2 else s_buf[p].at[:, s]
+
+    def build(p, s):
+        code = row_code(p)
+        width = PIECES[p][1]
+        hit = tab[p][s, 0:1, :] == code
+        for k in range(1, 4):
+            hit = hit | (tab[p][s, k : k + 1, :] == code)
+        pick = jnp.where(hit, 1.0, 0.0).astype(jnp.bfloat16)
+        rows = jnp.dot(pick, t[p][s], preferred_element_type=jnp.float32).astype(jnp.bfloat16)
+        rows_of(p, s)[...] = rows.reshape(4, 4, 16, width)
+
+    for p in range(3):
+        for c in tabs[p]:
+            c.wait_recv()
+        for s in (0, 3, 1):
+            build(p, s)
+    for p in range(3):
+        for c in twos[p]:
+            c.wait_recv()
+        build(p, 2)
+
+    second = {d: [] for d in ORDER}
+    for d in ORDER:
+        c = (4 - d) % 4
+        for b in (1, 3, 2):
+            o = 4 - b
+            second[d].append(go(s_buf[0].at[b, c], r2[0].at[o, c], "y", b))
+            second[d].append(go(s_buf[2].at[b, d], r2[2].at[o, d], "x", b))
+        if d:
+            second[d].append(go(s_buf[1].at[4 - d], r2[1].at[d], "z", 4 - d))
+
+    third = {}
+
+    def forward(d):
+        arrive(second[d])
+        cs = []
+        c0 = (4 - d) % 4
+        cs.append(go(r2[0].at[pl.ds(1, 3), c0], r3[0].at[d, pl.ds(1, 3)], "z", c0))
+        cs.append(go(s_buf[0].at[0, c0], r3[0].at[d, 0], "z", c0))
+        for c in (1, 3, 2, 0):
+            o = (4 - c) % 4
+            src = r2[1].at[d, c] if d else s_buf[1].at[0, c]
+            cs.append(go(src, r3[1].at[d, :, o], "x", c))
+            cs.append(go(r2[2].at[pl.ds(1, 3), d, c], r3[2].at[d, o, pl.ds(1, 3)], "y", c))
+            cs.append(go(s_buf[2].at[0, d, c], r3[2].at[d, o, 0], "y", c))
+        third[d] = cs
+
+    def experts(d):
+        arrive(third[d])
+        xs = [r3[p][d].reshape(256, PIECES[p][1]) for p in range(3)]
+
+        def step(i, _):
+            h = i // 3
+            at = (i % 3) * STEP
+
+            def side(start):
+                total = None
+                for p in range(3):
+                    lo, width = PIECES[p]
+                    w = gu[h, pl.ds(pl.multiple_of(start, 16), STEP), lo : lo + width]
+                    y = lax.dot_general(
+                        xs[p], w, (((1,), (1,)), ((), ())), preferred_element_type=jnp.float32
+                    )
+                    total = y if total is None else total + y
+                return total
+
+            gate, up = side(at), side(D // 4 + at)
+            act = (gate * (1.0 / (1.0 + jnp.exp(-1.702 * gate))) * (up + 1.0)).astype(jnp.bfloat16)
+            w = dn[h, pl.ds(pl.multiple_of(at, 16), STEP), :]
+            y = jnp.dot(act, w, preferred_element_type=jnp.float32)
+
+            @pl.when(i == 0)
+            def _():
+                ffn[...] = y
+
+            @pl.when(i > 0)
+            def _():
+                ffn[...] += y
+
+            return 0
+
+        lax.fori_loop(0, 6, step, 0)
+        for p in range(3):
+            lo, width = PIECES[p]
+            r3[p][d] = ffn[:, lo : lo + width].astype(jnp.bfloat16).reshape(4, 4, 16, width)
+
+    back3, back2 = {}, {}
+
+    def give_back(d):
+        cs, done = [], []
+        c0 = (4 - d) % 4
+        if d:
+            cs.append(go(r3[0].at[d, pl.ds(1, 3)], q3[0].at[pl.ds(1, 3), c0], "z", d))
+        done.append(go(r3[0].at[d, 0], q2[0].at[0, c0], "z", d))
+        for o in (1, 3, 2, 0):
+            c = (4 - o) % 4
+            if d == 0:
+                done.append(go(r3[1].at[d, :, o], q2[1].at[0, c], "x", o))
+            elif o:
+                cs.append(go(r3[1].at[d, :, o], q3[1].at[d, c], "x", o))
+            if o:
+                cs.append(go(r3[2].at[d, o, pl.ds(1, 3)], q3[2].at[pl.ds(1, 3), d, c], "y", o))
+            done.append(go(r3[2].at[d, o, 0], q2[2].at[0, d, c], "y", o))
+        back3[d] = cs
+        back2[d] = done
+
+    def hand_on(d):
+        arrive(back3[d])
+        cs = back2[d]
+        c0 = (4 - d) % 4
+        for o in (1, 3, 2):
+            b = 4 - o
+            src = q3[0].at[o, c0] if d else r3[0].at[0, o]
+            cs.append(go(src, q2[0].at[b, c0], "y", o))
+            cs.append(go(r3[2].at[d, 0, o], q2[2].at[b, d, 0], "x", o))
+            cs.append(go(q3[2].at[o, d, pl.ds(1, 3)], q2[2].at[b, d, pl.ds(1, 3)], "x", o))
+        if d:
+            cs.append(go(r3[1].at[d, :, 0], q2[1].at[4 - d, 0], "z", d))
+            cs.append(go(q3[1].at[d, pl.ds(1, 3)], q2[1].at[4 - d, pl.ds(1, 3)], "z", d))
+
+    forward(0)
+    forward(2)
+    for c in loads:
+        c.wait()
+    experts(0)
+    give_back(0)
+    forward(1)
+    forward(3)
+    experts(2)
+    give_back(2)
+    hand_on(0)
+    experts(1)
+    give_back(1)
+    hand_on(2)
+    experts(3)
+    give_back(3)
+    hand_on(1)
+    hand_on(3)
+    for d in ORDER:
+        arrive(back2[d])
+    cp.drain()
+    fetch = [copy(q2[p], s_buf[p]) for p in range(3)]
+    for c in fetch:
+        c.wait()
+
+    last = []
+
+    def combine(p, s):
+        code = row_code(p)
+        width = PIECES[p][1]
+        spread = jnp.zeros((256, TOK), jnp.float32)
+        for k in range(4):
+            spread = spread + jnp.where(
+                tab[p][s, k : k + 1, :] == code, tab[p][s, 4 + k : 5 + k, :], 0.0
+            )
+        high = spread.astype(jnp.bfloat16)
+        low = (spread - high.astype(jnp.float32)).astype(jnp.bfloat16)
+        rows = rows_of(p, s)[...].reshape(256, width)
+        over = (((0,), (0,)), ((), ()))
+        return lax.dot_general(
+            high, rows, over, preferred_element_type=jnp.float32
+        ) + lax.dot_general(low, rows, over, preferred_element_type=jnp.float32)
+
+    for s in (1, 3, 2):
+        for p in range(3):
+            part[p][s - 1] = combine(p, s).astype(jnp.bfloat16)
+            last.append(go(part[p].at[s - 1], got[p].at[3 - s], TURNS[p][0], s))
+    for p in range(3):
+        lo, width = PIECES[p]
+        acc[:, lo : lo + width] = residual[:, lo : lo + width].astype(jnp.float32) + combine(p, 0)
+    for c in last:
+        c.wait_recv()
+    for p in range(3):
+        lo, width = PIECES[p]
+        total = acc[:, lo : lo + width]
+        for i in range(3):
+            total = total + got[p][i].astype(jnp.float32)
+        out[:, lo : lo + width] = total.astype(jnp.bfloat16)
+    for c in last:
+        c.wait_send()
+
+
+def moe(table, moe_in, residual, gu0, gu1, dn0, dn1):
+    vmem, anyspace = pl.BlockSpec(memory_space=pltpu.VMEM), pl.BlockSpec(memory_space=pl.ANY)
+    bf = jnp.bfloat16
+    widths = [w for _, w in PIECES]
+    far = [jax.ShapeDtypeStruct((4, 4, 4, 16, w), bf) for w in widths] * 3
+    return pl.pallas_call(
+        moe_kernel,
+        out_shape=(jax.ShapeDtypeStruct((TOK, D), bf), *far),
+        in_specs=[vmem] * 3 + [anyspace] * 4,
+        out_specs=(vmem, *([anyspace] * 9)),
+        scratch_shapes=[
+            *(pltpu.VMEM((4, TOK, w), bf) for w in widths),
+            *(pltpu.VMEM((4, 4, 4, 16, w), bf) for w in widths),
+            *(pltpu.VMEM((4, 4, 4, 16, w), bf) for w in widths),
+            *(pltpu.VMEM((4, 8, TOK), jnp.float32) for w in widths),
+            *(pltpu.VMEM((3, TOK, w), bf) for w in widths),
+            *(pltpu.VMEM((3, TOK, w), bf) for w in widths),
+            pltpu.VMEM((2, HALF_D, D), bf),
+            pltpu.VMEM((2, HALF_D // 2, D), bf),
+            pltpu.VMEM((256, D), jnp.float32),
+            pltpu.VMEM((TOK, D), jnp.float32),
+            pltpu.SemaphoreType.DMA((MOE_COPIES,)),
+            pltpu.SemaphoreType.DMA((MOE_COPIES,)),
+            pltpu.SemaphoreType.DMA((64,)),
+        ],
+        compiler_params=pltpu.CompilerParams(
+            collective_id=1, has_side_effects=True, vmem_limit_bytes=60 * 2**20
+        ),
+    )(table, moe_in, residual, gu0, gu1, dn0, dn1)[0]
+
+
+def route_table(ids, weights):
+    named = ids[:, :, None] == jnp.arange(64, dtype=jnp.int32)
+    member = jnp.any(named, axis=1).astype(jnp.bfloat16)
+    tok = jnp.arange(TOK, dtype=jnp.int32)
+    before = (tok[None, :] < tok[:, None]).astype(jnp.bfloat16)
+    slot = jnp.dot(before, member, preferred_element_type=jnp.float32)
+    slot_of = jnp.sum(jnp.where(named, slot[:, None, :], 0.0), axis=2)
+    code = ids.astype(jnp.float32) * 16.0 + slot_of
+    return jnp.concatenate([code, weights], axis=1).T
 
 
 def local(
-    queries,
-    key_rows,
-    value_matrix,
-    hidden,
-    out_weight,
-    norm_gain,
-    block_order,
-    expert_ids,
-    route_weights,
-    gate_up_weight,
-    down_weight,
+    queries, key_rows, value_matrix, hidden, out_weight, norm_gain, block_order,
+    expert_ids, route_weights, gate_up_weight, down_weight,
 ):
     gate_up_own, down_own = gate_up_weight[0].T, down_weight[0]
+    table = route_table(expert_ids[0], route_weights[0])
     residual, moe_in, gate_up_oth, down_oth = front(
         queries[0], key_rows[0], value_matrix[0], hidden[0], norm_gain[None], out_weight.T,
         block_order, gate_up_own, down_own,
     )
-    gate_up_own, gate_up_oth = gate_up_own.T, gate_up_oth.T
-    res_float = residual.astype(jnp.float32)
-
-    ids, weights = expert_ids[0], route_weights[0]
-    token_count = ids.shape[0]
-    named = ids[:, :, None] == jnp.arange(EXPERTS, dtype=jnp.int32)
-    member = jnp.any(named, axis=1)
-    weight_of = jnp.sum(jnp.where(named, weights[:, :, None], 0.0), axis=1)
-    tok = jnp.arange(token_count, dtype=jnp.int32)
-    before = (tok[None, :] < tok[:, None]).astype(jnp.bfloat16)
-    slot = jnp.dot(
-        before, member.astype(jnp.bfloat16), preferred_element_type=jnp.float32
-    ).astype(jnp.int32)
-    place = (
-        member.T[:, None, :]
-        & (slot.T[:, None, :] == jnp.arange(CAP, dtype=jnp.int32)[None, :, None])
-    ).reshape(EXPERTS * CAP, token_count)
-    picked = place.astype(jnp.bfloat16)
-    spread = jnp.where(
-        place, jnp.broadcast_to(weight_of.T[:, None, :], (EXPERTS, CAP, token_count)).reshape(EXPERTS * CAP, token_count), 0.0
-    )
-    high = spread.astype(jnp.bfloat16)
-    low = (spread - high.astype(jnp.float32)).astype(jnp.bfloat16)
-
-    outgoing = jnp.dot(picked, moe_in, preferred_element_type=jnp.float32).astype(jnp.bfloat16)
-    rows = lax.all_to_all(
-        outgoing.reshape(EXPERTS, CAP, D), CHIPS, split_axis=0, concat_axis=0, tiled=True
-    ).reshape(EXPERTS * CAP, D)
-
-    def half(gate_up, down):
-        gate_up_out = jnp.dot(rows, gate_up, preferred_element_type=jnp.float32)
-        n = gate_up.shape[1] // 2
-        gate, up = gate_up_out[:, :n], gate_up_out[:, n:]
-        act = (gate * jax.nn.sigmoid(1.702 * gate) * (up + 1.0)).astype(jnp.bfloat16)
-        return jnp.dot(act, down, preferred_element_type=jnp.float32)
-
-    result = (half(gate_up_own, down_own) + half(gate_up_oth, down_oth)).astype(jnp.bfloat16)
-    returned = lax.all_to_all(
-        result.reshape(EXPERTS, CAP, D), CHIPS, split_axis=0, concat_axis=0, tiled=True
-    ).reshape(EXPERTS * CAP, D)
-    mixed = jnp.einsum("st,sd->td", high, returned, preferred_element_type=jnp.float32) + jnp.einsum(
-        "st,sd->td", low, returned, preferred_element_type=jnp.float32
-    )
-    return (res_float + mixed).astype(jnp.bfloat16)[None]
+    return moe(table, moe_in, residual, gate_up_own, gate_up_oth, down_own, down_oth)[None]
 
 
 def solution(mesh):

time: 317 us -> 210 us (0.66); the launches traced: 311 us -> 210 us
  Pallas kernels: 50.4 us -> 197 us
  waiting for transfers between devices: 86.3 us -> 0 us
  blocking collectives: 80.5 us -> 0 us
  matrix products: 57.7 us -> 0.14 us
  local copies, waits for them, and re-layouts: 25 us -> 9.52 us
  starting transfers between devices: 9.51 us -> 0 us
    pallas_call x0 -> x1, Pallas kernels: none -> 146 us  [moe(): pl.pallas_call(moe_kernel, out_shape=(jax.ShapeDtypeStruct((TOK, D), bf),...]
    all_to_all x1 -> x0, waiting for transfers between devices: 86.3 us -> none  [local(): lax.all_to_all(result.reshape(EXPERTS, CAP, D), CHIPS, split_axis=0, conc...]
    all_to_all x1 -> x0, blocking collectives: 80.5 us -> none  [local(): lax.all_to_all(outgoing.reshape(EXPERTS, CAP, D), CHIPS, split_axis=0, co...]
    dot_general x8 -> x1, matrix products: 57.7 us -> 0.14 us  [route_table(): slot = jnp.dot(before, member, preferred_element_type=jnp.float32)]
    convert_element_type x2 -> x0, local copies, waits for them, and re-layouts: 16.8 us -> none  [the longest x1 8.51 us: local(): (half(gate_up_own, down_own) + half(gate_up_oth, down_oth)).astype(jnp.bf...]
    all_to_all x1 -> x0, starting transfers between devices: 9.51 us -> none  [local(): lax.all_to_all(result.reshape(EXPERTS, CAP, D), CHIPS, split_axis=0, conc...]
    unnamed x25 -> x15, local copies, waits for them, and re-layouts: 6.23 us -> 6.55 us
  transfers between devices with their start and end apart: 1 -> 0, of which waited for: 1 -> 0; matrix products, arithmetic and copies ran while one was open for 0% -> 0% of each run, Pallas kernels for 0% -> 0%
where the time goes in v3:
time: 210 us
  Pallas kernels  197 us (94%)
  local copies, waits for them, and re-layouts  9.52 us (5%)
  other arithmetic  3.51 us (2%)
    pallas_call x1, Pallas kernels, moe(): pl.pallas_call(moe_kernel, out_shape=(jax.ShapeDtypeStruct((TOK, D), bf),...  146 us
    pallas_call x1, Pallas kernels, front(): pl.pallas_call(front_kernel, out_shape=(jax.ShapeDtypeStruct((TOK, D), bf...  50.4 us
    unnamed x15, local copies, waits for them, and re-layouts  6.55 us

profile of v3, /device:TPU:58, one launch (start us, length us, event | category | flops | bytes accessed | tf_op | source)
XLA Modules:
  0.0 210.0 jit_solution(16364605410043105142)
XLA Ops:
  0.0 0.0 copy-start
  0.0 0.8 fusion
  0.8 0.7 broadcast_in_dim.24.gain
  1.5 0.1 fusion.1
  1.7 0.7 select_reduce_fusion
  2.4 0.7 multiply_add_fusion
  3.1 1.3 maximum_bitcast_fusion.table
  4.4 1.5 copy.16
  5.8 0.0 copy-done
  5.8 0.0 copy-start.3
  5.9 1.0 copy-done.3
  6.9 0.0 copy-start.4
  6.9 0.8 copy-done.4
  7.7 0.0 copy-start.5
  7.7 0.8 copy-done.5
  8.6 0.0 copy-start.6
  8.6 0.7 copy-done.6
  9.2 50.4 %shard_map.109 = (bf16[128,2880]{1,0:T(8,128)(2,1)S(1)}, bf16[128,2880]{1,0:T(8,128)(2,1)S(1)}, bf16[1440,2880]{1,0:T(8,128)(2,1)}, bf16[720,2880]{1,0:T(8,128)(2,1)}) custom-call(s32[16]{0:T(128)S(1)} %copy-done.6, bf16[128,2048]{1,0:T(8,128)(2,1)S(1)} %bitcast.18, bf16[128,256]{1,0:T(8,128)(2,1)S(1)} %bitcast.19, bf16[128,256]{1,0:T(8,128)(2,1)S(1)} %bitcast.20, ...), custom_call_target="tpu_custom_call" | custom-call | tf_op jit(solution)/shard_map/pallas_call | solution.py:249
  59.7 0.0 copy-start.1
  59.7 0.9 copy-done.1
  60.5 0.0 copy-start.2
  60.5 0.9 copy-done.2
  61.4 146.4 %shard_map.110 = (bf16[128,2880]{1,0:T(8,128)(2,1)}, bf16[4,4,4,16,1024]{4,3,2,1,0:T(8,128)(2,1)}, bf16[4,4,4,16,1024]{4,3,2,1,0:T(8,128)(2,1)}, bf16[4,4,4,16,8...) custom-call(f32[8,128]{1,0:T(8,128)} %maximum_bitcast_fusion.table, ...), custom_call_target="tpu_custom_call" | custom-call | tf_op jit(solution)/shard_map/pallas_call | solution.py:531
  207.8 2.3 %copy.17 = bf16[1,128,2880]{1,2,0:T(8,128)(2,1)} copy(bf16[1,128,2880]{2,1,0:T(8,128)(2,1)} %bitcast.25) | data formatting | bytes 1474560 | tf_op jit(solution)/shard_map/broadcast_in_dim | solution.py:578
Async XLA Ops:
  0.0 5.8 %copy-start = (bf16[256,2880]{0,1:T(8,128)(2,1)S(1)}, bf16[256,2880]{0,1:T(8,128)(2,1)}, u32[]{:S(2)}) copy-start(bf16[256,2880]{0,1:T(8,128)(2,1)} %param.15) | copy-start | bytes 4423684
  5.8 1.0 copy-start.3
  6.9 0.8 copy-start.4
  7.7 0.8 copy-start.5
  8.6 0.7 copy-start.6
  59.7 0.9 copy-start.1
  60.5 0.9 copy-start.2

commit v4 on v3

v4 whole, which is shorter than its diff:
```python
import functools
import jax
import jax.numpy as jnp
from jax import lax
from jax.experimental import pallas as pl
from jax.experimental.pallas import tpu as pltpu
from jax.sharding import Mesh, PartitionSpec as P

D = 2880
HALF_D = D // 2
HEAD = 64
TOK = 128
QUARTER = 240
Q_FIRST = 128
REST = HALF_D - 4 * QUARTER
AXES = ("y_hi", "x", "y_lo", "z", "core")
MESH = pl.DeviceIdType.MESH
PIECES = ((0, 1024), (1024, 1024), (2048, 832))
CTX = ("y_hi", "x")
EXP = ("y_lo", "z", "core")


def here():
    return {a: lax.axis_index(a) for a in AXES}


def moved(me, axis, by):
    to = dict(me)
    if axis == "y":
        y = (me["y_hi"] * 2 + me["y_lo"] + by) % 4
        to["y_hi"], to["y_lo"] = y // 2, y % 2
    else:
        to[axis] = (me[axis] + by) % 4
    return to


class Copies:
    def __init__(self, send, recv):
        self.send, self.recv, self.made = send, recv, []

    def go(self, src, dst, to):
        i = len(self.made)
        c = pltpu.make_async_remote_copy(
            src_ref=src, dst_ref=dst, send_sem=self.send.at[i], recv_sem=self.recv.at[i],
            device_id=to, device_id_type=MESH,
        )
        c.start()
        self.made.append(c)
        return c

    def drain(self):
        for c in self.made:
            c.wait_send()


def greet(peers):
    barrier = pltpu.get_barrier_semaphore()
    for peer in peers:
        pl.semaphore_signal(barrier, inc=1, device_id=peer, device_id_type=MESH)
    pl.semaphore_wait(barrier, len(peers))


FRONT_COPIES = 80


def front_kernel(
    order, q_in, k_in, v_in, hid_in, gain_in, ow, ids_in, weights_in, gu, dn,
    residual, moe0, moe1, moe2, table, gu_oth, dn_oth,
    q, hid, gain, ids, kv, w, att, acc, got, rows, res_out, m0, m1, m2, tab, send, recv, local_sem,
):
    me = here()
    cp = Copies(send, recv)
    near = []

    def copy(src, dst):
        c = pltpu.make_async_copy(src, dst, local_sem.at[len(near)])
        c.start()
        near.append(c)
        return c

    core = me["core"]
    base = pl.multiple_of(core * HALF_D, 16)
    kv_in = (copy(k_in, kv.at[0, :, pl.ds(0, 256)]), copy(v_in, kv.at[0, :, pl.ds(256, 256)]))
    q_copy = copy(q_in, q)
    ids_copy, weights_copy = copy(ids_in, ids), copy(weights_in, tab.at[pl.ds(4, 4)])
    hid_copy, gain_copy = copy(hid_in, hid), copy(gain_in, gain)
    own_w = copy(ow.at[pl.ds(base, HALF_D)], w.at[0])

    other = dict(me, core=1 - core)
    kv_mate = dict(me, y_hi=1 - me["y_hi"])
    w_mate = dict(me, y_hi=1 - me["y_hi"], y_lo=1 - me["y_lo"])
    xp, xm = moved(me, "x", 1), moved(me, "x", 3)
    zp, zm = moved(me, "z", 1), moved(me, "z", 3)
    z = me["z"]
    greet([other, kv_mate, w_mate, xp, xm, zp, zm])

    def quarter(t, part=None):
        start = REST + QUARTER * ((z + t) % 4)
        size = QUARTER
        if part == 0:
            size = Q_FIRST
        elif part == 1:
            start, size = start + Q_FIRST, QUARTER - Q_FIRST
        return pl.ds(pl.multiple_of(start, 16), size)

    own_q = ow.at[pl.ds(pl.multiple_of(base + REST + QUARTER * z, 16), QUARTER)]
    own_r = ow.at[pl.ds(base, REST)]
    rest = pl.ds(0, REST)
    rest_parts = (pl.ds(0, REST // 2), pl.ds(REST // 2, REST // 2))
    kv_parts = (pl.ds(0, 64), pl.ds(64, 64))
    q_parts = (quarter(0, 0), quarter(0, 1))
    zq, zq2 = {}, {}

    def z_first(slot):
        part = w.at[slot, quarter(0)]
        zq[slot] = (cp.go(part, part, zp), cp.go(part, part, zm))

    def z_second(slot):
        for c in zq[slot]:
            c.wait_recv()
        a, b = w.at[slot, quarter(3, 0)], w.at[slot, quarter(1, 1)]
        zq2[slot] = (cp.go(a, a, zp), cp.go(b, b, zm))

    def x_first(buf, slot, part):
        src = buf.at[slot, part]
        return cp.go(src, buf.at[slot + 3, part], xp), cp.go(src, buf.at[slot + 1, part], xm)

    def x_second(buf, d, firsts, parts):
        for c in firsts:
            c.wait_recv()
        return (
            cp.go(buf.at[4 * d + 3, parts[0]], buf.at[4 * d + 2, parts[0]], xp),
            cp.go(buf.at[4 * d + 1, parts[1]], buf.at[4 * d + 2, parts[1]], xm),
        )

    def arrive(cs):
        for c in cs:
            c.wait_recv()

    yq = cp.go(own_q, w.at[4, quarter(0)], w_mate)
    xq0 = (cp.go(own_q, w.at[3, quarter(0)], xp), cp.go(own_q, w.at[1, quarter(0)], xm))
    for c in kv_in:
        c.wait()
    ky = cp.go(kv.at[0], kv.at[4], kv_mate)
    swaps = [cp.go(gu, gu_oth, other), cp.go(dn, dn_oth, other)]
    yq.wait_recv()
    xq1 = x_first(w, 4, quarter(0))
    z_first(4)
    every = pl.ds(0, TOK)
    kx0 = x_first(kv, 0, every)
    x2q0 = x_second(w, 0, xq0, q_parts)
    z_first(3)
    z_first(1)
    ky.wait_recv()
    kx1 = x_first(kv, 4, every)
    x2q1 = x_second(w, 1, xq1, q_parts)
    z_first(7)
    z_first(5)
    kx20 = x_second(kv, 0, kx0, kv_parts)
    yr = [cp.go(own_r, w.at[4, rest], w_mate)]
    xr = (cp.go(own_r, w.at[3, rest], xp), cp.go(own_r, w.at[1, rest], xm))
    arrive(x2q0)
    z_first(2)
    kx21 = x_second(kv, 1, kx1, kv_parts)
    arrive(x2q1)
    z_first(6)
    z_second(4)

    ids_copy.wait()
    weights_copy.wait()
    expert = lax.broadcasted_iota(jnp.int32, (64, TOK), 0)
    hits = [ids[k : k + 1, :] == expert for k in range(4)]
    member = jnp.where(hits[0] | hits[1] | hits[2] | hits[3], 1.0, 0.0).astype(jnp.bfloat16)
    earlier = jnp.where(
        lax.broadcasted_iota(jnp.int32, (TOK, TOK), 0) < lax.broadcasted_iota(jnp.int32, (TOK, TOK), 1),
        1.0, 0.0,
    ).astype(jnp.bfloat16)
    place = jnp.dot(member, earlier, preferred_element_type=jnp.float32)
    for k in range(4):
        slot_of = jnp.sum(jnp.where(hits[k], place, 0.0), axis=0, keepdims=True)
        tab[k : k + 1, :] = ids[k : k + 1, :].astype(jnp.float32) * 16.0 + slot_of
    tab_out = copy(tab, table)

    hid_copy.wait()
    for lo in range(0, D, 128):
        n = min(128, D - lo)
        rows[:, lo : lo + n] = hid[lo : lo + n, :].astype(jnp.float32).T

    ctx = me["y_hi"] * 4 + me["x"]
    col = lax.broadcasted_iota(jnp.int32, (1, 1024), 1)
    key_pos = col % 64
    for slot in range(8):
        block = ((me["y_hi"] + slot // 4) % 2) * 4 + (me["x"] + slot % 4) % 4
        for h in (0, 1):
            key_pos = key_pos + jnp.where(
                col // 64 == 2 * slot + h, order[2 * block + h] * 64, 0
            )
    row = lax.broadcasted_iota(jnp.int32, (256, 1), 0) % TOK
    query_pos = row % 64 + jnp.where(row < 64, order[2 * ctx] * 64, order[2 * ctx + 1] * 64)
    bias = jnp.where(key_pos <= query_pos, 0.0, -1e30)
    q_copy.wait()
    arrive(kx20)
    arrive(kx21)

    def group(g):
        keys = kv[:, :, 64 * g : 64 * g + 64].reshape(1024, HEAD)
        values = kv[:, :, 256 + 64 * g : 256 + 64 * g + 64].reshape(1024, HEAD)

        def pair(i, _):
            lanes = pl.ds(pl.multiple_of((4 * g + i) * 128, 128), 128)
            two = q[:, lanes] * jnp.bfloat16(0.125)
            two = jnp.concatenate([two[:, :HEAD], two[:, HEAD:]], axis=0)
            s = lax.dot_general(
                two, keys, (((1,), (1,)), ((), ())), preferred_element_type=jnp.float32
            ) + bias
            p = jnp.exp(s - jnp.max(s, axis=1, keepdims=True))
            total = jnp.sum(p, axis=1, keepdims=True)
            o = jnp.dot(p.astype(jnp.bfloat16), values, preferred_element_type=jnp.float32)
            o = (o / total).astype(jnp.bfloat16)
            att[0, :, lanes] = jnp.concatenate([o[:TOK], o[TOK:]], axis=1)
            return 0

        lax.fori_loop(0, 4, pair, 0)

    group(0)
    z_second(3)
    z_second(1)
    x2r = x_second(w, 0, xr, rest_parts)
    yr.append(cp.go(w.at[3, rest], w.at[7, rest], w_mate))
    yr.append(cp.go(w.at[1, rest], w.at[5, rest], w_mate))
    group(1)
    z_second(7)
    z_second(5)
    arrive(x2r)
    yr.append(cp.go(w.at[2, rest], w.at[6, rest], w_mate))
    group(2)
    z_second(2)
    z_second(6)
    group(3)
    att_out = cp.go(att.at[0], att.at[1], other)
    own_w.wait()
    att_out.wait_recv()

    def project(slot, first=False):
        block = ((me["y_hi"] + slot // 4) % 2) * 4 + (me["x"] + slot % 4) % 4
        lanes = pl.ds(pl.multiple_of(block * 256, 256), 256)
        both = att[:, :, lanes].reshape(2 * TOK, 256)
        part = lax.dot_general(
            both, w[slot], (((1,), (1,)), ((), ())), preferred_element_type=jnp.float32
        ).reshape(2, TOK, HALF_D)
        acc[...] = part if first else acc[...] + part

    project(0, True)
    for slot in (3, 1, 4, 7, 5, 2, 6):
        arrive(zq2[slot])
        if slot >= 4:
            yr[{4: 0, 7: 1, 5: 2, 6: 3}[slot]].wait_recv()
        project(slot)
    back = cp.go(acc.at[1], got, other)
    gain_copy.wait()
    back.wait_recv()
    mine, theirs = acc[0], got[...]
    left = jnp.where(core == 0, mine, theirs)
    right = jnp.where(core == 0, theirs, mine)
    res = (rows[...] + jnp.concatenate([left, right], axis=1)).astype(jnp.bfloat16)
    res_out[...] = res
    outs = [copy(res_out, residual)]
    res = res.astype(jnp.float32)
    scale = lax.rsqrt(jnp.mean(res * res, axis=1, keepdims=True) + 1e-05)
    normed = (res * scale * gain[...].reshape(1, D)).astype(jnp.bfloat16)
    for (lo, width), m, o in zip(PIECES, (m0, m1, m2), (moe0, moe1, moe2), strict=True):
        m[...] = normed[:, lo : lo + width]
        outs.append(copy(m, o))
    for c in outs:
        c.wait()
    tab_out.wait()
    arrive(swaps)
    cp.drain()


def front(q, k, v, hidden_t, gain, ow_t, order, ids_t, weights_t, gu_t, dn):
    anyspace = pl.BlockSpec(memory_space=pl.ANY)
    bf = jnp.bfloat16
    pieces = [(TOK, width) for _, width in PIECES]
    return pl.pallas_call(
        front_kernel,
        out_shape=(
            jax.ShapeDtypeStruct((TOK, D), bf),
            *(jax.ShapeDtypeStruct(p, bf) for p in pieces),
            jax.ShapeDtypeStruct((8, TOK), jnp.float32),
            jax.ShapeDtypeStruct(gu_t.shape, bf), jax.ShapeDtypeStruct(dn.shape, bf),
        ),
        in_specs=[pl.BlockSpec(memory_space=pltpu.SMEM)] + [anyspace] * 10,
        out_specs=(anyspace,) * 7,
        scratch_shapes=[
            pltpu.VMEM((TOK, 2048), bf),
            pltpu.VMEM((D, TOK), bf),
            pltpu.VMEM((D,), jnp.float32),
            pltpu.VMEM((4, TOK), jnp.int32),
            pltpu.VMEM((8, TOK, 512), bf),
            pltpu.VMEM((8, HALF_D, 256), bf),
            pltpu.VMEM((2, TOK, 2048), bf),
            pltpu.VMEM((2, TOK, HALF_D), jnp.float32),
            pltpu.VMEM((TOK, HALF_D), jnp.float32),
            pltpu.VMEM((TOK, D), jnp.float32),
            pltpu.VMEM((TOK, D), bf),
            *(pltpu.VMEM(p, bf) for p in pieces),
            pltpu.VMEM((8, TOK), jnp.float32),
            pltpu.SemaphoreType.DMA((FRONT_COPIES,)),
            pltpu.SemaphoreType.DMA((FRONT_COPIES,)),
            pltpu.SemaphoreType.DMA((16,)),
        ],
        compiler_params=pltpu.CompilerParams(
            collective_id=0, has_side_effects=True, vmem_limit_bytes=60 * 2**20
        ),
    )(order, q, k, v, hidden_t, gain, ow_t, ids_t, weights_t, gu_t, dn)


TURNS = (("x", "y", "z"), ("y", "z", "x"), ("z", "x", "y"))
ORDER = (0, 2, 1, 3)
MOE_COPIES = 200
FF_HALF = 720


def moe_kernel(
    table, in0, in1, in2, residual, gu0, gu1, dn0, dn1,
    out, *refs,
):
    r2, q3 = refs[0:3], refs[3:6]
    t, s_buf, r3, q2, tab, part, got = (refs[6 + 3 * i : 9 + 3 * i] for i in range(7))
    gu, dn, act, res, send, recv, local_sem = refs[27:]
    me = here()
    cp = Copies(send, recv)
    near = []

    def copy(src, dst):
        c = pltpu.make_async_copy(src, dst, local_sem.at[len(near)])
        c.start()
        near.append(c)
        return c

    def go(src, dst, axis, by):
        if by == 0:
            return copy(src, dst)
        return cp.go(src, dst, moved(me, axis, by))

    def arrive(cs):
        for c in cs:
            if any(c is n for n in near):
                c.wait()
            else:
                c.wait_recv()

    tab_in = [copy(table, tab[p].at[0]) for p in range(3)]
    own_in = [copy(src, t[p].at[0]) for p, src in enumerate((in0, in1, in2))]
    loads = [copy(gu0, gu.at[0]), copy(gu1, gu.at[1]), copy(dn0, dn.at[0]), copy(dn1, dn.at[1])]
    res_in = copy(residual, res)
    greet([moved(me, a, by) for a in ("x", "y", "z") for by in (1, 3, 2)])

    tabs, ones, twos = {}, {}, {}
    for p in range(3):
        a = TURNS[p][0]
        tab_in[p].wait()
        tabs[p] = [go(tab[p].at[0], tab[p].at[4 - by], a, by) for by in (1, 3, 2)]
    for p in range(3):
        a = TURNS[p][0]
        own_in[p].wait()
        ones[p] = (go(t[p].at[0], t[p].at[3], a, 1), go(t[p].at[0], t[p].at[1], a, 3))

    row = lax.broadcasted_iota(jnp.int32, (256, 1), 0)
    y_me = me["y_hi"] * 2 + me["y_lo"]

    def row_code(p):
        at = {"x": me["x"], "y": y_me, "z": me["z"]}
        _, b, c = TURNS[p]
        at[b] = (at[b] + row // 64) % 4
        at[c] = (at[c] + (row // 16) % 4) % 4
        expert = (at["y"] // 2) * 32 + at["x"] * 8 + (at["y"] % 2) * 4 + at["z"]
        return (expert * 16 + row % 16).astype(jnp.float32)

    def rows_of(bufs, p, s):
        return bufs[p].at[:, :, s] if p < 2 else bufs[p].at[:, s]

    def build(p, s):
        code = row_code(p)
        width = PIECES[p][1]
        hit = tab[p][s, 0:1, :] == code
        for k in range(1, 4):
            hit = hit | (tab[p][s, k : k + 1, :] == code)
        pick = jnp.where(hit, 1.0, 0.0).astype(jnp.bfloat16)
        rows = jnp.dot(pick, t[p][s], preferred_element_type=jnp.float32).astype(jnp.bfloat16)
        rows_of(s_buf, p, s)[...] = rows.reshape(4, 4, 16, width)

    second = {d: [] for d in ORDER}

    def second_two(d):
        for b in (1, 3, 2):
            second[d].append(go(s_buf[2].at[b, d], r2[2].at[4 - b, d], "x", b))

    build(2, 0)
    second_two(0)
    build(0, 0)
    build(1, 0)
    halves = (pl.ds(0, 64), pl.ds(64, 64))
    for p in range(3):
        a = TURNS[p][0]
        arrive(ones[p])
        twos[p] = (
            go(t[p].at[3, halves[0]], t[p].at[2, halves[0]], a, 1),
            go(t[p].at[1, halves[1]], t[p].at[2, halves[1]], a, 3),
        )
    for p in (2, 0, 1):
        arrive(tabs[p])
        for s in (3, 1):
            build(p, s)
    for p in (0, 1, 2):
        arrive(twos[p])
        build(p, 2)
    for d in ORDER:
        c = (4 - d) % 4
        for b in (1, 3, 2):
            second[d].append(go(s_buf[0].at[b, c], r2[0].at[4 - b, c], "y", b))
        if d:
            second_two(d)
            second[d].append(go(s_buf[1].at[4 - d], r2[1].at[d], "z", 4 - d))

    third = {}

    def forward(d):
        arrive(second[d])
        cs = []
        c0 = (4 - d) % 4
        cs.append(go(r2[0].at[pl.ds(1, 3), c0], r3[0].at[d, pl.ds(1, 3)], "z", c0))
        cs.append(go(s_buf[0].at[0, c0], r3[0].at[d, 0], "z", c0))
        for c in (1, 3, 2, 0):
            o = (4 - c) % 4
            src = r2[1].at[d, c] if d else s_buf[1].at[0, c]
            cs.append(go(src, r3[1].at[d, :, o], "x", c))
            cs.append(go(r2[2].at[pl.ds(1, 3), d, c], r3[2].at[d, o, pl.ds(1, 3)], "y", c))
            cs.append(go(s_buf[2].at[0, d, c], r3[2].at[d, o, 0], "y", c))
        third[d] = cs

    back3, back2 = {}, {}

    def give_back(d, p):
        cs, done = [], []
        c0 = (4 - d) % 4
        if p == 0:
            if d:
                cs.append(go(r3[0].at[d, pl.ds(1, 3)], q3[0].at[pl.ds(1, 3), c0], "z", d))
            done.append(go(r3[0].at[d, 0], q2[0].at[0, c0], "z", d))
        for o in (1, 3, 2, 0):
            c = (4 - o) % 4
            if p == 1:
                if d == 0:
                    done.append(go(r3[1].at[d, :, o], q2[1].at[0, c], "x", o))
                elif o:
                    cs.append(go(r3[1].at[d, :, o], q3[1].at[d, c], "x", o))
            elif p == 2:
                if o:
                    cs.append(go(r3[2].at[d, o, pl.ds(1, 3)], q3[2].at[pl.ds(1, 3), d, c], "y", o))
                done.append(go(r3[2].at[d, o, 0], q2[2].at[0, d, c], "y", o))
        back3[p, d] = cs
        back2[p, d] = done

    def hand_on(d):
        c0 = (4 - d) % 4
        arrive(back3[0, d])
        for o in (1, 3, 2):
            src = q3[0].at[o, c0] if d else r3[0].at[0, o]
            back2[0, d].append(go(src, q2[0].at[4 - o, c0], "y", o))
        arrive(back3[1, d])
        if d:
            back2[1, d].append(go(r3[1].at[d, :, 0], q2[1].at[4 - d, 0], "z", d))
            back2[1, d].append(
                go(q3[1].at[d, pl.ds(1, 3)], q2[1].at[4 - d, pl.ds(1, 3)], "z", d)
            )
        arrive(back3[2, d])
        for o in (1, 3, 2):
            b = 4 - o
            back2[2, d].append(go(r3[2].at[d, 0, o], q2[2].at[b, d, 0], "x", o))
            back2[2, d].append(
                go(q3[2].at[o, d, pl.ds(1, 3)], q2[2].at[b, d, pl.ds(1, 3)], "x", o)
            )

    def experts(d, between):
        arrive(third[d])
        xs = [r3[p][d].reshape(256, PIECES[p][1]) for p in range(3)]

        def first(h, _):
            def side(start):
                total = None
                for p in range(3):
                    lo, width = PIECES[p]
                    y = lax.dot_general(
                        xs[p], gu[h, start : start + FF_HALF, lo : lo + width],
                        (((1,), (1,)), ((), ())), preferred_element_type=jnp.float32,
                    )
                    total = y if total is None else total + y
                return total

            gate, up = side(0), side(FF_HALF)
            act[h] = (gate * (1.0 / (1.0 + jnp.exp(-1.702 * gate))) * (up + 1.0)).astype(jnp.bfloat16)
            return 0

        lax.fori_loop(0, 2, first, 0)
        between()
        for p in range(3):
            lo, width = PIECES[p]
            y = jnp.dot(
                act[0], dn[0, :, lo : lo + width], preferred_element_type=jnp.float32
            ) + jnp.dot(act[1], dn[1, :, lo : lo + width], preferred_element_type=jnp.float32)
            r3[p][d] = y.astype(jnp.bfloat16).reshape(4, 4, 16, width)
            give_back(d, p)

    last = []

    def combine(p, s):
        code = row_code(p)
        width = PIECES[p][1]
        spread = jnp.zeros((256, TOK), jnp.float32)
        for k in range(4):
            spread = spread + jnp.where(
                tab[p][s, k : k + 1, :] == code, tab[p][s, 4 + k : 5 + k, :], 0.0
            )
        high = spread.astype(jnp.bfloat16)
        low = (spread - high.astype(jnp.float32)).astype(jnp.bfloat16)
        rows = rows_of(q2, p, s)[...].reshape(256, width)
        over = (((0,), (0,)), ((), ()))
        return lax.dot_general(
            high, rows, over, preferred_element_type=jnp.float32
        ) + lax.dot_general(low, rows, over, preferred_element_type=jnp.float32)

    def hand_in(p, s):
        part[p][s - 1] = combine(p, s).astype(jnp.bfloat16)
        last.append(go(part[p].at[s - 1], got[p].at[3 - s], TURNS[p][0], s))

    forward(0)
    forward(2)
    for c in loads:
        c.wait()
    experts(0, lambda: forward(1))
    experts(2, lambda: (forward(3), hand_on(0)))
    experts(1, lambda: hand_on(2))
    experts(3, lambda: hand_on(1))
    arrive(back2[2, 2])
    hand_in(2, 2)
    hand_on(3)
    arrive(back2[2, 1])
    hand_in(2, 1)
    for p in (0, 1):
        for d in ORDER:
            arrive(back2[p, d])
        for s in (1, 3, 2):
            hand_in(p, s)
    arrive(back2[2, 3])
    hand_in(2, 3)
    arrive(back2[2, 0])
    res_in.wait()
    owns = []
    for p in range(3):
        lo, width = PIECES[p]
        owns.append(res[:, lo : lo + width].astype(jnp.float32) + combine(p, 0))
    for c in last:
        c.wait_recv()
    for p in range(3):
        lo, width = PIECES[p]
        total = owns[p]
        for i in range(3):
            total = total + got[p][i].astype(jnp.float32)
        for at in range(0, width, 128):
            n = min(128, width - at)
            out[lo + at : lo + at + n, :] = total[:, at : at + n].T.astype(jnp.bfloat16)
    cp.drain()


def moe(table, pieces, residual, gu0, gu1, dn0, dn1):
    vmem, anyspace = pl.BlockSpec(memory_space=pltpu.VMEM), pl.BlockSpec(memory_space=pl.ANY)
    bf = jnp.bfloat16
    widths = [w for _, w in PIECES]
    far = [jax.ShapeDtypeStruct((4, 4, 4, 16, w), bf) for w in widths] * 2
    return pl.pallas_call(
        moe_kernel,
        out_shape=(jax.ShapeDtypeStruct((D, TOK), bf), *far),
        in_specs=[anyspace] * 9,
        out_specs=(vmem, *([anyspace] * 6)),
        scratch_shapes=[
            *(pltpu.VMEM((4, TOK, w), bf) for w in widths),
            *(pltpu.VMEM((4, 4, 4, 16, w), bf) for w in widths * 3),
            *(pltpu.VMEM((4, 8, TOK), jnp.float32) for w in widths),
            *(pltpu.VMEM((3, TOK, w), bf) for w in widths),
            *(pltpu.VMEM((3, TOK, w), bf) for w in widths),
            pltpu.VMEM((2, HALF_D, D), bf),
            pltpu.VMEM((2, FF_HALF, D), bf),
            pltpu.VMEM((2, 256, FF_HALF), bf),
            pltpu.VMEM((TOK, D), bf),
            pltpu.SemaphoreType.DMA((MOE_COPIES,)),
            pltpu.SemaphoreType.DMA((MOE_COPIES,)),
            pltpu.SemaphoreType.DMA((64,)),
        ],
        compiler_params=pltpu.CompilerParams(
            collective_id=1, has_side_effects=True, vmem_limit_bytes=60 * 2**20
        ),
    )(table, *pieces, residual, gu0, gu1, dn0, dn1)[0]


def local(
    queries, key_rows, value_matrix, hidden, out_weight, norm_gain, block_order,
    expert_ids, route_weights, gate_up_weight, down_weight,
):
    gate_up_own, down_own = gate_up_weight[0].T, down_weight[0]
    residual, *pieces, table, gate_up_oth, down_oth = front(
        queries[0], key_rows[0], value_matrix[0], hidden[0].T, norm_gain, out_weight.T,
        block_order, expert_ids[0].T, route_weights[0].T, gate_up_own, down_own,
    )
    return moe(table, pieces, residual, gate_up_own, gate_up_oth, down_own, down_oth).T[None]


def solution(mesh):
    fine = Mesh(mesh.devices.reshape(2, 4, 2, 4, 2), ("y_hi", "x", "y_lo", "z", "core"))
    rows = P(EXP, CTX, None)
    halves = P(CTX + EXP, None, None)
    return jax.shard_map(
        local,
        mesh=fine,
        in_specs=(
            rows, rows, rows, rows, P(CTX, None), P(), P(), rows, rows, halves, halves,
        ),
        out_specs=rows,
        check_vma=False,
    )
```

time: 210 us -> 221 us (1.052); the launches traced: 210 us -> 219 us
  Pallas kernels: 197 us -> 216 us
  local copies, waits for them, and re-layouts: 9.52 us -> 2.03 us
  other arithmetic: 3.51 us -> 0 us
    pallas_call x1, Pallas kernels: 146 us -> 160 us  [moe(): pl.pallas_call(moe_kernel, out_shape=(jax.ShapeDtypeStruct((D, TOK), bf),...]
    pallas_call x1, Pallas kernels: 50.4 us -> 56.7 us  [front(): pl.pallas_call(front_kernel, out_shape=(jax.ShapeDtypeStruct((TOK, D), bf...]
    unnamed x15 -> x1, local copies, waits for them, and re-layouts: 6.55 us -> 2.03 us
    broadcast_in_dim x2 -> x0, local copies, waits for them, and re-layouts: 2.98 us -> none  [the longest x1 2.26 us: local(): moe(table, moe_in, residual, gate_up_own, gate_up_oth, down_own, down_oth)]
where the time goes in v4:
time: 221 us; the launch traced here: 219 us
  Pallas kernels  216 us (98%)
    pallas_call x1, Pallas kernels, moe(): pl.pallas_call(moe_kernel, out_shape=(jax.ShapeDtypeStruct((D, TOK), bf),...  160 us
    pallas_call x1, Pallas kernels, front(): pl.pallas_call(front_kernel, out_shape=(jax.ShapeDtypeStruct((TOK, D), bf...  56.7 us

profile of v4, /device:TPU:58, one launch (start us, length us, event | category | flops | bytes accessed | tf_op | source)
XLA Modules:
  0.0 218.5 jit_solution(3084321880512943874)
XLA Ops:
  0.0 56.7 %shard_map.109 = (bf16[128,2880]{1,0:T(8,128)(2,1)}, bf16[128,1024]{1,0:T(8,128)(2,1)}, bf16[128,1024]{1,0:T(8,128)(2,1)}, bf16[128,832]{1,0:T(8,128)(2,1)}, f32...) custom-call(s32[16]{0:T(128)} %order.1, bf16[128,2048]{1,0:T(8,128)(2,1)} %bitcast.27, ...), custom_call_target="tpu_custom_call" | custom-call | tf_op jit(solution)/shard_map/pallas_call | solution.py:285
  56.7 159.8 %shard_map.110 = (bf16[2880,128]{1,0:T(8,128)(2,1)}, bf16[4,4,4,16,1024]{4,3,2,1,0:T(8,128)(2,1)}, bf16[4,4,4,16,1024]{4,3,2,1,0:T(8,128)(2,1)}, bf16[4,4,4,16,8...) custom-call(f32[8,128]{1,0:T(8,128)} %get-tuple-element.13.table, ...), custom_call_target="tpu_custom_call" | custom-call | tf_op jit(solution)/shard_map/pallas_call | solution.py:582
  216.5 2.0 copy.13

commit v5 on v4

--- a/solution.py
+++ b/solution.py
@@ -10,8 +10,8 @@
 HALF_D = D // 2
 HEAD = 64
 TOK = 128
-QUARTER = 240
-Q_FIRST = 128
+QUARTER = 224
+Q_FIRST = 112
 REST = HALF_D - 4 * QUARTER
 AXES = ("y_hi", "x", "y_lo", "z", "core")
 MESH = pl.DeviceIdType.MESH
@@ -142,12 +142,14 @@
     for c in kv_in:
         c.wait()
     ky = cp.go(kv.at[0], kv.at[4], kv_mate)
+    every = pl.ds(0, TOK)
+    kx0 = x_first(kv, 0, every)
+    yr = [cp.go(own_r, w.at[4, rest], w_mate)]
+    xr = (cp.go(own_r, w.at[3, rest], xp), cp.go(own_r, w.at[1, rest], xm))
     swaps = [cp.go(gu, gu_oth, other), cp.go(dn, dn_oth, other)]
     yq.wait_recv()
     xq1 = x_first(w, 4, quarter(0))
     z_first(4)
-    every = pl.ds(0, TOK)
-    kx0 = x_first(kv, 0, every)
     x2q0 = x_second(w, 0, xq0, q_parts)
     z_first(3)
     z_first(1)
@@ -157,14 +159,14 @@
     z_first(7)
     z_first(5)
     kx20 = x_second(kv, 0, kx0, kv_parts)
-    yr = [cp.go(own_r, w.at[4, rest], w_mate)]
-    xr = (cp.go(own_r, w.at[3, rest], xp), cp.go(own_r, w.at[1, rest], xm))
     arrive(x2q0)
     z_first(2)
     kx21 = x_second(kv, 1, kx1, kv_parts)
     arrive(x2q1)
     z_first(6)
     z_second(4)
+    arrive(yr)
+    xr1 = x_first(w, 4, rest)
 
     ids_copy.wait()
     weights_copy.wait()
@@ -223,16 +225,13 @@
         lax.fori_loop(0, 4, pair, 0)
 
     group(0)
+    x2r0 = x_second(w, 0, xr, rest_parts)
     z_second(3)
     z_second(1)
-    x2r = x_second(w, 0, xr, rest_parts)
-    yr.append(cp.go(w.at[3, rest], w.at[7, rest], w_mate))
-    yr.append(cp.go(w.at[1, rest], w.at[5, rest], w_mate))
     group(1)
     z_second(7)
     z_second(5)
-    arrive(x2r)
-    yr.append(cp.go(w.at[2, rest], w.at[6, rest], w_mate))
+    x2r1 = x_second(w, 1, xr1, rest_parts)
     group(2)
     z_second(2)
     z_second(6)
@@ -253,8 +252,8 @@
     project(0, True)
     for slot in (3, 1, 4, 7, 5, 2, 6):
         arrive(zq2[slot])
-        if slot >= 4:
-            yr[{4: 0, 7: 1, 5: 2, 6: 3}[slot]].wait_recv()
+        if slot in (2, 6):
+            arrive(x2r0 if slot == 2 else x2r1)
         project(slot)
     back = cp.go(acc.at[1], got, other)
     gain_copy.wait()
@@ -397,10 +396,6 @@
         for b in (1, 3, 2):
             second[d].append(go(s_buf[2].at[b, d], r2[2].at[4 - b, d], "x", b))
 
-    build(2, 0)
-    second_two(0)
-    build(0, 0)
-    build(1, 0)
     halves = (pl.ds(0, 64), pl.ds(64, 64))
     for p in range(3):
         a = TURNS[p][0]
@@ -409,19 +404,19 @@
             go(t[p].at[3, halves[0]], t[p].at[2, halves[0]], a, 1),
             go(t[p].at[1, halves[1]], t[p].at[2, halves[1]], a, 3),
         )
-    for p in (2, 0, 1):
+    for p in range(3):
         arrive(tabs[p])
-        for s in (3, 1):
+        for s in (0, 3, 1):
             build(p, s)
-    for p in (0, 1, 2):
+    for p in range(3):
         arrive(twos[p])
         build(p, 2)
     for d in ORDER:
         c = (4 - d) % 4
         for b in (1, 3, 2):
             second[d].append(go(s_buf[0].at[b, c], r2[0].at[4 - b, c], "y", b))
+        second_two(d)
         if d:
-            second_two(d)
             second[d].append(go(s_buf[1].at[4 - d], r2[1].at[d], "z", 4 - d))
 
     third = {}
@@ -483,7 +478,7 @@
                 go(q3[2].at[o, d, pl.ds(1, 3)], q2[2].at[b, d, pl.ds(1, 3)], "x", o)
             )
 
-    def experts(d, between):
+    def experts(d):
         arrive(third[d])
         xs = [r3[p][d].reshape(256, PIECES[p][1]) for p in range(3)]
 
@@ -504,7 +499,6 @@
             return 0
 
         lax.fori_loop(0, 2, first, 0)
-        between()
         for p in range(3):
             lo, width = PIECES[p]
             y = jnp.dot(
@@ -537,25 +531,24 @@
 
     forward(0)
     forward(2)
+    forward(1)
+    forward(3)
     for c in loads:
         c.wait()
-    experts(0, lambda: forward(1))
-    experts(2, lambda: (forward(3), hand_on(0)))
-    experts(1, lambda: hand_on(2))
-    experts(3, lambda: hand_on(1))
-    arrive(back2[2, 2])
-    hand_in(2, 2)
+    experts(0)
+    experts(2)
+    hand_on(0)
+    experts(1)
+    hand_on(2)
+    experts(3)
+    hand_on(1)
     hand_on(3)
-    arrive(back2[2, 1])
-    hand_in(2, 1)
-    for p in (0, 1):
+    for p in range(3):
         for d in ORDER:
             arrive(back2[p, d])
-        for s in (1, 3, 2):
+    for s in (1, 3, 2):
+        for p in range(3):
             hand_in(p, s)
-    arrive(back2[2, 3])
-    hand_in(2, 3)
-    arrive(back2[2, 0])
     res_in.wait()
     owns = []
     for p in range(3):

time: 221 us -> 184 us (0.83)
  Pallas kernels: 216 us -> 179 us
    pallas_call x1, Pallas kernels: 160 us -> 127 us  [moe(): pl.pallas_call(moe_kernel, out_shape=(jax.ShapeDtypeStruct((D, TOK), bf),...]
    pallas_call x1, Pallas kernels: 56.7 us -> 51.5 us  [front(): pl.pallas_call(front_kernel, out_shape=(jax.ShapeDtypeStruct((TOK, D), bf...]
where the time goes in v5:
time: 184 us; the launch traced here: 181 us
  Pallas kernels  179 us (97%)
  local copies, waits for them, and re-layouts  2.03 us (1%)
    pallas_call x1, Pallas kernels, moe(): pl.pallas_call(moe_kernel, out_shape=(jax.ShapeDtypeStruct((D, TOK), bf),...  127 us
    pallas_call x1, Pallas kernels, front(): pl.pallas_call(front_kernel, out_shape=(jax.ShapeDtypeStruct((TOK, D), bf...  51.5 us

profile of v5, /device:TPU:58, one launch (start us, length us, event | category | flops | bytes accessed | tf_op | source)
XLA Modules:
  0.0 180.7 jit_solution(1658053835079503430)
XLA Ops:
  0.0 51.5 %shard_map.109 = (bf16[128,2880]{1,0:T(8,128)(2,1)}, bf16[128,1024]{1,0:T(8,128)(2,1)}, bf16[128,1024]{1,0:T(8,128)(2,1)}, bf16[128,832]{1,0:T(8,128)(2,1)}, f32...) custom-call(s32[16]{0:T(128)} %order.1, bf16[128,2048]{1,0:T(8,128)(2,1)} %bitcast.27, ...), custom_call_target="tpu_custom_call" | custom-call | tf_op jit(solution)/shard_map/pallas_call | solution.py:284
  51.5 127.2 %shard_map.110 = (bf16[2880,128]{1,0:T(8,128)(2,1)}, bf16[4,4,4,16,1024]{4,3,2,1,0:T(8,128)(2,1)}, bf16[4,4,4,16,1024]{4,3,2,1,0:T(8,128)(2,1)}, bf16[4,4,4,16,8...) custom-call(f32[8,128]{1,0:T(8,128)} %get-tuple-element.13.table, ...), custom_call_target="tpu_custom_call" | custom-call | tf_op jit(solution)/shard_map/pallas_call | solution.py:575
  178.7 2.0 %copy.13 = bf16[1,128,2880]{1,2,0:T(8,128)(2,1)} copy(bf16[1,128,2880]{1,2,0:T(8,128)(2,1)} %bitcast.25) | data formatting | bytes 1474560

commit v6 on v5

--- a/solution.py
+++ b/solution.py
@@ -137,13 +137,13 @@
         for c in cs:
             c.wait_recv()
 
-    yq = cp.go(own_q, w.at[4, quarter(0)], w_mate)
-    xq0 = (cp.go(own_q, w.at[3, quarter(0)], xp), cp.go(own_q, w.at[1, quarter(0)], xm))
     for c in kv_in:
         c.wait()
     ky = cp.go(kv.at[0], kv.at[4], kv_mate)
     every = pl.ds(0, TOK)
     kx0 = x_first(kv, 0, every)
+    yq = cp.go(own_q, w.at[4, quarter(0)], w_mate)
+    xq0 = (cp.go(own_q, w.at[3, quarter(0)], xp), cp.go(own_q, w.at[1, quarter(0)], xm))
     yr = [cp.go(own_r, w.at[4, rest], w_mate)]
     xr = (cp.go(own_r, w.at[3, rest], xp), cp.go(own_r, w.at[1, rest], xm))
     swaps = [cp.go(gu, gu_oth, other), cp.go(dn, dn_oth, other)]
@@ -224,21 +224,30 @@
 
         lax.fori_loop(0, 4, pair, 0)
 
+    att_out = []
+
+    def share(g):
+        lanes = pl.ds(512 * g, 512)
+        att_out.append(cp.go(att.at[0, :, lanes], att.at[1, :, lanes], other))
+
     group(0)
+    share(0)
     x2r0 = x_second(w, 0, xr, rest_parts)
     z_second(3)
     z_second(1)
     group(1)
+    share(1)
     z_second(7)
     z_second(5)
     x2r1 = x_second(w, 1, xr1, rest_parts)
     group(2)
+    share(2)
     z_second(2)
     z_second(6)
     group(3)
-    att_out = cp.go(att.at[0], att.at[1], other)
+    share(3)
     own_w.wait()
-    att_out.wait_recv()
+    arrive(att_out)
 
     def project(slot, first=False):
         block = ((me["y_hi"] + slot // 4) % 2) * 4 + (me["x"] + slot % 4) % 4
@@ -316,7 +325,7 @@
 
 
 TURNS = (("x", "y", "z"), ("y", "z", "x"), ("z", "x", "y"))
-ORDER = (0, 2, 1, 3)
+ORDER = (0, 1, 3, 2)
 MOE_COPIES = 200
 FF_HALF = 720
 
@@ -530,24 +539,23 @@
         last.append(go(part[p].at[s - 1], got[p].at[3 - s], TURNS[p][0], s))
 
     forward(0)
-    forward(2)
     forward(1)
     forward(3)
+    forward(2)
     for c in loads:
         c.wait()
     experts(0)
-    experts(2)
+    experts(1)
     hand_on(0)
-    experts(1)
-    hand_on(2)
     experts(3)
     hand_on(1)
+    experts(2)
     hand_on(3)
+    hand_on(2)
     for p in range(3):
         for d in ORDER:
             arrive(back2[p, d])
-    for s in (1, 3, 2):
-        for p in range(3):
+        for s in (1, 3, 2):
             hand_in(p, s)
     res_in.wait()
     owns = []

time: 184 us -> 186 us (1.011); the launches traced: 181 us -> 185 us
  Pallas kernels: 179 us -> 183 us
    pallas_call x1, Pallas kernels: 127 us -> 133 us  [moe(): pl.pallas_call(moe_kernel, out_shape=(jax.ShapeDtypeStruct((D, TOK), bf),...]
where the time goes in v6:
time: 186 us; the launch traced here: 185 us
  Pallas kernels  183 us (98%)
  local copies, waits for them, and re-layouts  2.03 us (1%)
    pallas_call x1, Pallas kernels, moe(): pl.pallas_call(moe_kernel, out_shape=(jax.ShapeDtypeStruct((D, TOK), bf),...  133 us
    pallas_call x1, Pallas kernels, front(): pl.pallas_call(front_kernel, out_shape=(jax.ShapeDtypeStruct((TOK, D), bf...  50.5 us

profile of v6, /device:TPU:58, one launch (start us, length us, event | category | flops | bytes accessed | tf_op | source)
XLA Modules:
  0.0 185.3 jit_solution(1323547033529159819)
XLA Ops:
  0.0 50.5 %shard_map.109 = (bf16[128,2880]{1,0:T(8,128)(2,1)}, bf16[128,1024]{1,0:T(8,128)(2,1)}, bf16[128,1024]{1,0:T(8,128)(2,1)}, bf16[128,832]{1,0:T(8,128)(2,1)}, f32...) custom-call(s32[16]{0:T(128)} %order.1, bf16[128,2048]{1,0:T(8,128)(2,1)} %bitcast.27, ...), custom_call_target="tpu_custom_call" | custom-call | tf_op jit(solution)/shard_map/pallas_call | solution.py:293
  50.5 132.8 %shard_map.110 = (bf16[2880,128]{1,0:T(8,128)(2,1)}, bf16[4,4,4,16,1024]{4,3,2,1,0:T(8,128)(2,1)}, bf16[4,4,4,16,1024]{4,3,2,1,0:T(8,128)(2,1)}, bf16[4,4,4,16,8...) custom-call(f32[8,128]{1,0:T(8,128)} %get-tuple-element.13.table, ...), custom_call_target="tpu_custom_call" | custom-call | tf_op jit(solution)/shard_map/pallas_call | solution.py:583
  183.3 2.0 %copy.13 = bf16[1,128,2880]{1,2,0:T(8,128)(2,1)} copy(bf16[1,128,2880]{1,2,0:T(8,128)(2,1)} %bitcast.25) | data formatting | bytes 1474560
